TPU v7x, 512 devices: a whole 4x4x16 slice. The times are simulated.
512 devices in a mesh: cols: 32 (over z, core), rep: 16 (over y, x).
Axes of the slice: x: 4, y: 4, z: 16, core: 2. Of those that a mesh axis runs over, the one named last changes fastest.
Arguments:
- hamiltonian_band: float32 [64, 5, 128, 128], P('cols'), may hold values from -0.25 to 0.25
- margin_factors: float32 [64, 256, 128], P('cols', 'rep'), may hold values from -0.25 to 0.25
- neighbour_mask: int32 [64, 5], P('cols'), may hold values from 0 to 1, as said below
- fermi_level: float32 [1], replicated, may hold values from -0.3 to 0.3
Outputs:
- density: float32 [64, 640, 640], P('cols', 'rep')
Inputs may be any that keep to these rules, and one draw needn't show every extreme that they name: `neighbour_mask`: entry 2 of every row is 1; every row has 3 to 5 ones; some row has 5 ones and some row has exactly 3.
All inputs are finite; a program needn't handle non-finite values.
Results may differ from a plain program's by a relative error of at most 0.0003.
Values sent between devices are 32-bit elements; how exact they have to be, the bound alone decides.
A program may use at most 64 MiB of HBM per device.

v0:
```python
import jax
import jax.numpy as jnp
from jax import lax
from jax.sharding import PartitionSpec as P

B = 128
W = 2
SIGN = 2
NC = 5


def extended(block, sides, width):
    for axis, dim in sides:
        count = lax.axis_size(axis)
        forward = [(i, i + 1) for i in range(count - 1)]
        forward.append((count - 1, 0))
        backward = [(target, source) for source, target in forward]
        low = lax.ppermute(
            lax.slice_in_dim(block, block.shape[dim] - width, None, axis=dim), axis, forward
        )
        high = lax.ppermute(lax.slice_in_dim(block, 0, width, axis=dim), axis, backward)
        block = jnp.concatenate([low, block, high], axis=dim)
    return block


def batched(left, right):
    return jnp.einsum(
        "cij,cjk->cik",
        left,
        right,
        preferred_element_type=jnp.float32,
        precision=lax.Precision.HIGHEST,
    )


def assemble(band, local_mask, col_count):
    block_rows = []
    for left_idx in range(NC):
        block_line = []
        for right_idx in range(NC):
            if abs(left_idx - right_idx) <= W:
                first = band[right_idx : right_idx + col_count, left_idx - right_idx + W]
                second = band[left_idx : left_idx + col_count, W - left_idx + right_idx]
                weight = local_mask[:, left_idx] * local_mask[:, right_idx]
                block_line.append(
                    0.5 * (first + jnp.swapaxes(second, 1, 2)) * weight[:, None, None]
                )
            else:
                block_line.append(jnp.zeros((col_count, B, B), jnp.float32))
        block_rows.append(jnp.concatenate(block_line, axis=2))
    return jnp.concatenate(block_rows, axis=1)


def on_device(hamiltonian_band, margin_factors, neighbour_mask, fermi_level):
    col_count = hamiltonian_band.shape[0]
    width = NC * B
    rep_size = lax.axis_size("rep")
    rep_index = lax.axis_index("rep")
    piece_height = width // rep_size
    first_row = rep_index * piece_height
    local_mask = neighbour_mask.astype(jnp.float32)
    identity = jnp.eye(width, dtype=jnp.float32)
    identity_part = lax.dynamic_slice_in_dim(identity, first_row, piece_height, 0)
    widened = extended(margin_factors, (("cols", 0),), W)
    stacked = jnp.concatenate(
        [widened[idx : idx + col_count] * local_mask[:, idx][:, None, None] for idx in range(NC)],
        axis=2,
    )
    partial_gram = jnp.einsum(
        "cpi,cpj->cij",
        stacked,
        stacked,
        preferred_element_type=jnp.float32,
        precision=lax.Precision.HIGHEST,
    )
    gram_full = lax.psum(partial_gram, "rep")
    margin = identity + gram_full
    band = extended(hamiltonian_band, (("cols", 0),), W)
    hamilton = assemble(band, local_mask, col_count)
    root_scale = 2.0 * jnp.sqrt(jnp.sum(margin * margin, axis=(1, 2)) / width)
    forward_iter = margin / root_scale[:, None, None]
    forward_rows = lax.dynamic_slice_in_dim(forward_iter, first_row, piece_height, 1)
    step_part = 0.5 * (3.0 * identity_part - forward_rows)
    forward_part = batched(step_part, forward_iter)
    inverse_part = step_part
    forward_iter = lax.all_gather(forward_part, "rep", axis=1, tiled=True)
    inverse_iter = lax.all_gather(inverse_part, "rep", axis=1, tiled=True)
    inverse_rows = lax.dynamic_slice_in_dim(inverse_iter, first_row, piece_height, 1)
    step_part = 0.5 * (3.0 * identity_part - batched(inverse_rows, forward_iter))
    inverse_part = batched(step_part, inverse_iter)
    inverse_part = inverse_part / jnp.sqrt(root_scale)[:, None, None]
    inverse_full = lax.all_gather(inverse_part, "rep", axis=1, tiled=True)
    ortho_part = batched(batched(inverse_part, hamilton), inverse_full)
    shifted = ortho_part - fermi_level[0] * identity_part
    total_sq = lax.psum(jnp.sum(shifted * shifted, axis=(1, 2)), "rep")
    spread = 2.0 * jnp.sqrt(total_sq / width + 1e-05)
    sign_part = shifted / spread[:, None, None]
    for iteration in range(SIGN):
        sign_full = lax.all_gather(sign_part, "rep", axis=1, tiled=True)
        square_part = batched(sign_part, sign_full)
        cube_part = batched(square_part, sign_full)
        sign_part = 0.5 * (3.0 * sign_part - cube_part)
    return 0.5 * (identity_part - sign_part)


def solution(mesh):
    in_specs = (P("cols", None, None, None), P("cols", "rep", None), P("cols", None), P())
    out_specs = P("cols", "rep", None)
    return jax.shard_map(
        on_device, mesh=mesh, in_specs=in_specs, out_specs=out_specs, check_vma=False
    )
```

profile of v0, /device:TPU:1, one launch (start us, length us, event | category | flops | bytes accessed | tf_op | source)
XLA Modules:
  0.0 542.8 jit_solution(2152616024105681856)
XLA Ops:
  6.5 3.0 collective-permute-start
  9.6 3.8 collective-permute-start.1
  13.4 0.7 convert_element_type.13
  14.1 0.3 slice_reduce_fusion
  14.4 0.8 constant_dynamic-update-slice_fusion.3
  15.2 0.8 constant_dynamic-update-slice_fusion.2
  16.0 0.8 constant_dynamic-update-slice_fusion.1
  16.8 4.5 fusion.36
  22.1 0.7 broadcast_multiply_fusion.1
  22.8 127.4 %all-reduce.2.cloned.1.call-done = f32[2,640,640]{2,1,0:T(8,128)} async-done(((f32[2,640,640]{2,1,0:T(8,128)}), f32[2,640,640]{2,1,0:T(8,128)}) %all-reduce.2.cloned.1.call-update) | async-done | bytes 3276816 | tf_op jit(solution)/shard_map/psum | solution.py:76
  150.2 2.6 multiply_reduce_fusion
  152.8 0.3 copy-done.2
  153.1 0.4 add_divide_fusion
  153.5 1.7 copy-done
  155.2 4.6 fusion.37
  159.9 0.7 all-gather.6.cloned.1.call-update
  160.7 0.9 copy.5
  161.5 2.3 collective-permute-start.2
  164.1 58.3 %all-gather.8.cloned.1.call-done = f32[2,640,640]{2,1,0:T(8,128)} async-done(((f32[2,40,640]{2,1,0:T(8,128)}), f32[2,640,640]{2,1,0:T(8,128)}) %all-gather.8.cloned.1.call-update) | async-done | bytes 3276816 | tf_op jit(solution)/shard_map/all_gather | solution.py:86
  222.4 65.5 %all-gather.6.cloned.1.call-done = f32[2,640,640]{2,1,0:T(8,128)} async-done(((f32[2,40,640]{2,1,0:T(8,128)}), f32[2,640,640]{2,1,0:T(8,128)}) %all-gather.6.cloned.1.call-update) | async-done | bytes 3276816 | tf_op jit(solution)/shard_map/all_gather | solution.py:87
  287.9 4.1 fusion.4
  292.0 2.6 convolution_divide_fusion
  294.8 0.8 copy.20
  295.6 0.8 copy.21
  296.4 0.6 multiply_multiply_fusion
  297.0 0.7 copy.10
  297.7 0.7 copy.6
  298.7 1.1 copy-done.8
  299.8 0.7 slice_bitcast_fusion
  300.5 1.8 bitcast_add_fusion.10
  302.3 1.7 copy.11
  304.0 0.7 copy.19
  304.7 1.7 copy.13
  306.4 0.8 copy.15
  307.1 0.8 copy.18
  307.9 0.8 pad_maximum_fusion.1
  308.7 0.7 copy.23
  309.4 1.7 copy.25
  311.1 0.7 copy.26
  311.8 0.8 copy.27
  312.6 0.7 copy.28
  313.5 1.1 fusion.29
  314.7 1.0 maximum_dynamic-update-slice_fusion.1
  315.7 0.9 constant_dynamic-update-slice_fusion.7
  316.6 1.0 fusion.28
  317.6 1.0 multiply_dynamic-update-slice_fusion.2
  318.8 1.0 fusion.22
  320.1 1.0 fusion.16
  321.1 1.0 fusion.14
  322.3 1.7 copy-done.5
  324.1 1.0 copy.31
  325.3 0.9 maximum_dynamic-update-slice_fusion
  326.2 3.8 fusion.38
  330.0 27.1 %all-gather.10.cloned.1.call-done = f32[2,640,640]{2,1,0:T(8,128)} async-done(((f32[2,40,640]{2,1,0:T(8,128)}), f32[2,640,640]{2,1,0:T(8,128)}) %all-gather.10.cloned.1.call-update) | async-done | bytes 3276816 | tf_op jit(solution)/shard_map/all_gather | solution.py:92
  357.1 3.9 multiply_reduce_fusion.1
  361.0 30.9 %psum.15 = f32[2]{0:T(128)S(1)} all-reduce(f32[2]{0:T(128)S(1)} %get-tuple-element.48), channel_id=1, replica_groups=mesh['cols'=32,'rep'=16] {'rep'}, use_global_device_ids=true, to_apply=%region_3.0 | all-reduce | flops 2 | bytes 16 | tf_op jit(solution)/shard_map/psum | solution.py:95
  391.9 0.8 broadcast_divide_fusion
  392.7 0.3 all-gather.14.cloned.1.call-start
  393.0 67.1 %all-gather.12.cloned.1.call-done = f32[2,640,640]{2,1,0:T(8,128)} async-done(((f32[2,40,640]{2,1,0:T(8,128)}), f32[2,640,640]{2,1,0:T(8,128)}) %all-gather.12.cloned.1.call-update) | async-done | bytes 3276816 | tf_op jit(solution)/shard_map/all_gather | solution.py:99
  460.1 4.1 fusion.39
  464.2 2.6 broadcast_multiply_fusion
  466.8 62.5 %all-gather.14.cloned.1.call-done = f32[2,640,640]{2,1,0:T(8,128)} async-done(((f32[2,40,640]{2,1,0:T(8,128)}), f32[2,640,640]{2,1,0:T(8,128)}) %all-gather.14.cloned.1.call-update) | async-done | bytes 3276816 | tf_op jit(solution)/shard_map/all_gather | solution.py:99
  529.4 4.0 fusion.35
  533.4 2.6 fusion.3
  (77 shorter events, 2.3 us)
Async XLA Ops:
  6.5 143.7 %all-reduce.2.cloned.1.call-start = ((), (), s32[]{:S(2)}) async-start(), calls=%async_computation | async-start | bytes 6553600 | tf_op jit(solution)/shard_map/psum | solution.py:76
  6.5 7.8 %collective-permute-start = (f32[2,16,128]{2,1,0:T(8,128)}, f32[2,16,128]{2,1,0:T(8,128)S(1)}, u32[]{:S(2)}, u32[]{:S(2)}) collective-permute-start(f32[2,16,128]{2,1,0:T(8,128)} %param.5), channel_id=1, source_target_pairs={{0,16},{16,32},{32,48},{48,64},{64,80},{80,96},{96,112},{112,128},... | collective-permute-start | bytes 49160 | tf_op jit(solution)/shard_map/ppermute | solution.py:18
  9.6 6.4 %collective-permute-start.1 = (f32[2,16,128]{2,1,0:T(8,128)}, f32[2,16,128]{2,1,0:T(8,128)S(1)}, u32[]{:S(2)}, u32[]{:S(2)}) collective-permute-start(f32[2,16,128]{2,1,0:T(8,128)} %param.5), channel_id=1, source_target_pairs={{16,0},{32,16},{48,32},{64,48},{80,64},{96,80},{112,96},{128,112},... | collective-permute-start | bytes 49160 | tf_op jit(solution)/shard_map/ppermute | solution.py:21
  21.3 201.1 %all-gather.8.cloned.1.call-start = ((), (), s32[]{:S(2)}) async-start(), calls=%async_computation.2 | async-start | bytes 3481600 | tf_op jit(solution)/shard_map/all_gather | solution.py:86
  150.2 2.9 copy-start.2
  153.5 1.7 copy-start
  155.2 5.5 %copy-start.4 = (f32[2,5,128,128]{3,2,1,0:T(8,128)S(1)}, f32[2,5,128,128]{3,2,1,0:T(8,128)}, u32[]{:S(2)}) copy-start(f32[2,5,128,128]{3,2,1,0:T(8,128)} %param.4) | copy-start | bytes 1966084
  155.2 4.7 copy-start.9
  159.9 128.0 %all-gather.6.cloned.1.call-start = ((), (), s32[]{:S(2)}) async-start(), calls=%async_computation.1 | async-start | bytes 3481600 | tf_op jit(solution)/shard_map/all_gather | solution.py:87
  160.6 196.5 %all-gather.10.cloned.1.call-start = ((), (), s32[]{:S(2)}) async-start(), calls=%async_computation.3 | async-start | bytes 3481600 | tf_op jit(solution)/shard_map/all_gather | solution.py:92
  161.5 135.4 %collective-permute-start.2 = (f32[2,5,128,128]{3,2,0,1:T(8,128)}, f32[2,5,128,128]{3,2,0,1:T(8,128)S(1)}, u32[]{:S(2)}, u32[]{:S(2)}) collective-permute-start(f32[2,5,128,128]{3,2,0,1:T(8,128)} %copy.5), channel_id=1, source_target_pairs={{0,16},{16,32},{32,48},{48,64},{64,80},{80,96},{96,112},{112,128},... | collective-permute-start | bytes 1966088 | tf_op jit(solution)/shard_map/ppermute | solution.py:18
  164.1 136.5 %collective-permute-start.3 = (f32[2,5,128,128]{2,3,0,1:T(8,128)S(1)}, f32[2,5,128,128]{2,3,0,1:T(8,128)S(1)}, u32[]{:S(2)}, u32[]{:S(2)}) collective-permute-start(f32[2,5,128,128]{2,3,0,1:T(8,128)S(1)} %copy.14), channel_id=1, source_target_pairs={{16,0},{32,16},{48,32},{64,48},{80,64},{96,80},{112,96},{128,112},... | collective-permute-start | bytes 1966088 | tf_op jit(solution)/shard_map/ppermute | solution.py:21
  287.9 4.1 copy-start.6
  294.6 165.5 %all-gather.12.cloned.1.call-start = ((), (), s32[]{:S(2)}) async-start(), calls=%async_computation.4 | async-start | bytes 3481600 | tf_op jit(solution)/shard_map/all_gather | solution.py:99
  298.7 1.1 copy-start.8
  313.4 5.2 copy-start.17
  313.4 5.3 copy-start.13
  313.4 6.4 %copy-start.12 = (f32[2,128,128]{1,2,0:T(8,128)S(1)}, f32[2,128,128]{1,2,0:T(8,128)}, u32[]{:S(2)}) copy-start(f32[2,128,128]{1,2,0:T(8,128)} %copy.21) | copy-start | bytes 393220
  313.5 6.4 %copy-start.16 = (f32[2,128,128]{2,1,0:T(8,128)S(1)}, f32[2,128,128]{2,1,0:T(8,128)}, u32[]{:S(2)}) copy-start(f32[2,128,128]{2,1,0:T(8,128)} %copy.23) | copy-start | bytes 393220
  313.5 6.5 %copy-start.15 = (f32[2,128,128]{2,1,0:T(8,128)S(1)}, f32[2,128,128]{2,1,0:T(8,128)}, u32[]{:S(2)}) copy-start(f32[2,128,128]{2,1,0:T(8,128)} %copy.25) | copy-start | bytes 393220
  313.5 8.6 %copy-start.14 = (f32[2,128,128]{2,1,0:T(8,128)S(1)}, f32[2,128,128]{2,1,0:T(8,128)}, u32[]{:S(2)}) copy-start(f32[2,128,128]{2,1,0:T(8,128)} %copy.27) | copy-start | bytes 393220
  314.6 7.6 %copy-start.11 = (f32[2,128,128]{2,1,0:T(8,128)S(1)}, f32[2,128,128]{2,1,0:T(8,128)}, u32[]{:S(2)}) copy-start(f32[2,128,128]{2,1,0:T(8,128)} %copy.28) | copy-start | bytes 393220
  320.0 6.2 %copy-start.10 = (f32[2,40,640]{2,1,0:T(8,128)S(1)}, f32[2,40,640]{2,1,0:T(8,128)}, u32[]{:S(2)}) copy-start(f32[2,40,640]{2,1,0:T(8,128)} %convolution_divide_fusion) | copy-start | bytes 614404
  322.3 1.7 copy-start.5
  324.1 33.0 %copy-start.18 = (f32[40,640]{1,0:T(8,128)S(1)}, f32[40,640]{1,0:T(8,128)}, u32[]{:S(2)}) copy-start(f32[40,640]{1,0:T(8,128)} %get-tuple-element.10) | copy-start | bytes 307204
  392.7 71.5 %copy-start.7 = (f32[2,40,640]{2,1,0:T(8,128)S(1)}, f32[2,40,640]{2,1,0:T(8,128)}, u32[]{:S(2)}) copy-start(f32[2,40,640]{2,1,0:T(8,128)} %broadcast_divide_fusion) | copy-start | bytes 614404
  392.7 136.6 %all-gather.14.cloned.1.call-start = ((), (), s32[]{:S(2)}) async-start(), calls=%async_computation.5 | async-start | bytes 3481600 | tf_op jit(solution)/shard_map/all_gather | solution.py:99
  460.1 4.1 copy-start.3
  529.4 4.0 copy-start.1
Sparse Core Ops, SparseCore 0:
  21.4 128.7 all-reduce.1
  160.0 62.3 all-gather.7
  225.5 62.3 all-gather.5
  294.7 62.3 all-gather.9
  392.8 67.2 all-gather.11
  466.9 62.3 all-gather.13
where the time goes:
time: 543 us
  waiting for transfers between devices  409 us (75%)
  matrix products  36.7 us (7%)
  blocking collectives  30.9 us (6%)
  local copies, waits for them, and re-layouts  22.5 us (4%)
  other arithmetic  19.6 us (4%)
  between operations  14.6 us (3%)
  starting transfers between devices  9.79 us (2%)
    all_gather x2, waiting for transfers between devices, on_device(): sign_full = lax.all_gather(sign_part, 'rep', axis=1, tiled=True)  130 us
    psum x1, waiting for transfers between devices, on_device(): gram_full = lax.psum(partial_gram, 'rep')  127 us
    all_gather x1, waiting for transfers between devices, on_device(): inverse_iter = lax.all_gather(inverse_part, 'rep', axis=1, tiled=True)  65.5 us
    all_gather x1, waiting for transfers between devices, on_device(): forward_iter = lax.all_gather(forward_part, 'rep', axis=1, tiled=True)  58.3 us
    dot_general x9, matrix products, batched(): jnp.einsum('cij,cjk->cik', left, right, preferred_element_type=jnp.float3...  32.3 us
    psum x1, blocking collectives, on_device(): total_sq = lax.psum(jnp.sum(shifted * shifted, axis=(1, 2)), 'rep')  30.9 us
    all_gather x1, waiting for transfers between devices, on_device(): inverse_full = lax.all_gather(inverse_part, 'rep', axis=1, tiled=True)  27.1 us
  transfers between devices with their start and end apart: 10, of which 6 were waited for; matrix products, arithmetic and copies ran while one was open for 8% of the time, Pallas kernels for 0%

commit v1 on v0

v1 whole, which is shorter than its diff:
```python
import functools
import jax, jax.numpy as jnp
from jax import lax
from jax.experimental import pallas as pl
from jax.experimental.pallas import tpu as pltpu
B=128; NC=5; M=640; PS=256; ROWS=80
F32=jnp.float32; BF=jnp.bfloat16

def split(x):
    hi = x.astype(BF)
    return hi, (x - hi.astype(F32)).astype(BF)

def dot(a, b):
    return jnp.dot(a, b, preferred_element_type=F32)

def dot_nt(a, b):
    return lax.dot_general(a, b, (((1,), (1,)), ((), ())), preferred_element_type=F32)

def dot3(a, b, d=dot):
    (ah, al), (bh, bl) = a, b
    return d(ah, bh) + d(ah, bl) + d(al, bh)

def rows_kernel(mask_ref, fermi_ref, row_ref, y_ref, hb_ref, out_ref, h_ref, yt_ref, x_ref, lw_ref, rw_ref):
    for a in range(NC):
        blk = y_ref[a] * mask_ref[a]
        yt_ref[a*B:(a+1)*B, :] = blk.T
    yt = split(yt_ref[...])
    y_full = jnp.concatenate([y_ref[a] * mask_ref[a] for a in range(NC)], axis=1)
    y = split(y_full)
    for a in range(NC):
        for b in range(NC):
            sl = (slice(a*B, (a+1)*B), slice(b*B, (b+1)*B))
            if abs(a-b) <= 2:
                w = 0.5 * mask_ref[a] * mask_ref[b]
                h_ref[sl] = (hb_ref[b, a-b+2] + hb_ref[a, b-a+2].T) * w
            else:
                h_ref[sl] = jnp.zeros((B, B), F32)
    eye = (lax.broadcasted_iota(jnp.int32, (PS, PS), 0) == lax.broadcasted_iota(jnp.int32, (PS, PS), 1))
    k = dot3(y, yt)
    one = jnp.ones((1, 1), F32)
    sumsq = M * one + 2.0 * jnp.sum(jnp.where(eye, k, 0.0), keepdims=True) + jnp.sum(k*k, keepdims=True)
    c = 2.0 * jnp.sqrt(sumsq / M)
    al = 1.0 / c
    t = 0.5 * (3.0 - al)
    u = 0.5 * (3.0 - al * t * t)
    ks = split(k)
    k2 = dot3(ks, ks)
    b0 = al * t * (t - al); b1 = al * al * (0.25 * al - t); b2 = 0.25 * al * al * al
    bm = b1 * k + b2 * k2 + jnp.where(eye, b0, 0.0)
    kb = dot3(ks, split(bm))
    rs = lax.rsqrt(c)
    rm = (-0.5 * t * bm + 0.25 * al * kb - jnp.where(eye, 0.5 * al * u, 0.0)) * rs
    a0 = t * u * rs
    vt = dot3(yt, split(rm))
    vts = split(vt)
    pt = dot3(split(h_ref[...]), yt)
    n = dot3(y, split(pt))
    pt2 = a0 * pt + 0.5 * dot3(vts, split(n))
    w = dot3(split(pt2), vts, dot_nt)
    x_ref[...] = w
    mu = fermi_ref[0]
    a2 = a0 * a0
    acc = jnp.zeros((1, 1), F32)
    for a in range(NC):
        for b in range(NC):
            sl = (slice(a*B, (a+1)*B), slice(b*B, (b+1)*B))
            e = x_ref[sl] + x_ref[sl[1], sl[0]].T
            if abs(a-b) <= 2:
                e = e + a2 * h_ref[sl]
            if a == b:
                ey = (lax.broadcasted_iota(jnp.int32, (B, B), 0) == lax.broadcasted_iota(jnp.int32, (B, B), 1))
                e = e - jnp.where(ey, mu, 0.0)
            acc = acc + jnp.sum(e * e, keepdims=True)
            h_ref[sl] = e
    inv = 1.0 / (2.0 * jnp.sqrt(acc / M + 1e-5))
    x0 = h_ref[...] * inv
    xh, xl = split(x0)
    lw_ref[:, 0:M] = xh; lw_ref[:, M:2*M] = xl; lw_ref[:, 2*M:3*M] = xh
    rw_ref[0:M, :] = xh; rw_ref[M:2*M, :] = xh; rw_ref[2*M:3*M, :] = xl
    a_m = dot(lw_ref[...], rw_ref[...])
    ah, alo = split(a_m)
    rw_ref[0:M, :] = ah; rw_ref[M:2*M, :] = ah; rw_ref[2*M:3*M, :] = alo
    x1 = 1.5 * x0 - 0.5 * dot(lw_ref[...], rw_ref[...])
    x_ref[...] = x1
    xh, xl = split(x1)
    rw_ref[0:M, :] = xh; rw_ref[M:2*M, :] = xh; rw_ref[2*M:3*M, :] = xl
    r0 = pl.multiple_of(row_ref[0], 8)
    xr = x_ref[pl.ds(r0, ROWS), :]
    rh, rl = split(xr)
    q = dot(jnp.concatenate([rh, rl, rh], axis=1), rw_ref[...])
    qh, ql = split(q)
    cube = dot(jnp.concatenate([qh, ql, qh], axis=1), rw_ref[...])
    x2 = 1.5 * xr - 0.5 * cube
    ii = lax.broadcasted_iota(jnp.int32, (ROWS, M), 0) + r0
    jj = lax.broadcasted_iota(jnp.int32, (ROWS, M), 1)
    out_ref[...] = jnp.where(ii == jj, 0.5, 0.0) - 0.5 * x2

def rows_call(mask, fermi, row, y, hb):
    vm = pl.BlockSpec(memory_space=pltpu.VMEM); sm = pl.BlockSpec(memory_space=pltpu.SMEM)
    return pl.pallas_call(rows_kernel, out_shape=jax.ShapeDtypeStruct((ROWS, M), F32),
        in_specs=[sm, sm, sm, vm, vm], out_specs=vm,
        scratch_shapes=[pltpu.VMEM((M, M), F32), pltpu.VMEM((M, PS), F32), pltpu.VMEM((M, M), F32),
            pltpu.VMEM((M, 3*M), BF), pltpu.VMEM((3*M, M), BF)],
        compiler_params=pltpu.CompilerParams(vmem_limit_bytes=50<<20))(mask, fermi, row, y, hb)


from jax.sharding import PartitionSpec as P

def extended(block, axis="cols"):
    n = lax.axis_size(axis)
    fwd = [(i, (i + 1) % n) for i in range(n)]
    bwd = [(d, s) for s, d in fwd]
    low = lax.ppermute(block, axis, fwd)
    high = lax.ppermute(block, axis, bwd)
    return jnp.concatenate([low, block, high], axis=0)

def on_device(hamiltonian_band, margin_factors, neighbour_mask, fermi_level):
    rep = lax.axis_index("rep")
    g = rep % 2
    wide = extended(margin_factors)
    y = lax.all_gather(wide, "rep", axis=1, tiled=True)
    y = lax.dynamic_slice_in_dim(y, g, NC, 0)
    hb = lax.dynamic_slice_in_dim(extended(hamiltonian_band), g, NC, 0)
    mask = lax.dynamic_slice_in_dim(neighbour_mask, g, 1, 0)[0].astype(F32)
    row = (rep // 2) * ROWS
    rows = rows_call(mask, fermi_level, row[None].astype(jnp.int32), y, hb)
    first, second = rows[:40], rows[40:]
    keep = jnp.where(g == 0, first, second)
    send = jnp.where(g == 0, second, first)
    n = lax.axis_size("rep")
    got = lax.ppermute(send, "rep", [(i, i ^ 1) for i in range(n)])
    return jnp.stack([jnp.where(g == 0, keep, got), jnp.where(g == 0, got, keep)])

def solution(mesh):
    in_specs = (P("cols", None, None, None), P("cols", "rep", None), P("cols", None), P())
    return jax.shard_map(on_device, mesh=mesh, in_specs=in_specs, out_specs=P("cols", "rep", None), check_vma=False)
```

time: 543 us -> 62.4 us (0.11)
  the two profiles are of different devices: /device:TPU:1 before, /device:TPU:2 now
where the time goes in v1:
time: 62.4 us; the launch traced here: 62.1 us
  blocking collectives  24.4 us (39%)
  starting transfers between devices  14.6 us (23%)
  Pallas kernels  11.6 us (19%)
  waiting for transfers between devices  8.27 us (13%)
  other arithmetic  2.51 us (4%)
  between operations  0.72 us (1%)
    all_gather x1, blocking collectives, on_device(): y = lax.all_gather(wide, 'rep', axis=1, tiled=True)  24.4 us
    ppermute x2, starting transfers between devices, extended(): high = lax.ppermute(block, axis, bwd)  11.9 us
    pallas_call x1, Pallas kernels, rows_call(): pl.pallas_call(rows_kernel, out_shape=jax.ShapeDtypeStruct((ROWS, M), F32...  11.6 us
    ppermute x2, waiting for transfers between devices, extended(): low = lax.ppermute(block, axis, fwd)  4.42 us
    ppermute x1, waiting for transfers between devices, on_device(): got = lax.ppermute(send, 'rep', [(i, i ^ 1) for i in range(n)])  3.85 us
    ppermute x1, starting transfers between devices, on_device(): got = lax.ppermute(send, 'rep', [(i, i ^ 1) for i in range(n)])  2.7 us
  transfers between devices with their start and end apart: 5, of which 2 were waited for; matrix products, arithmetic and copies ran while one was open for 2% of the time, Pallas kernels for 0%

profile of v1, /device:TPU:2, one launch (start us, length us, event | category | flops | bytes accessed | tf_op | source)
XLA Modules:
  0.0 62.1 jit_solution(2961806702246026682)
XLA Ops:
  0.0 0.0 copy-start
  0.0 0.0 collective-permute-start.2
  0.0 8.9 %collective-permute-start.3 = (f32[2,5,128,128]{3,2,1,0:T(8,128)}, f32[2,5,128,128]{3,2,1,0:T(8,128)S(1)}, u32[]{:S(2)}, u32[]{:S(2)}) collective-permute-start(f32[2,5,128,128]{3,2,1,0:T(8,128)} %param.4), channel_id=1, source_target_pairs={{16,0},{32,16},{48,32},{64,48},{80,64},{96,80},{112,96},{128,112},... | collective-permute-start | bytes 1966088 | tf_op jit(solution)/shard_map/ppermute | solution.py:114
  8.9 0.0 collective-permute-start
  9.0 3.0 %collective-permute-start.1 = (f32[2,16,128]{2,1,0:T(8,128)}, f32[2,16,128]{2,1,0:T(8,128)S(1)}, u32[]{:S(2)}, u32[]{:S(2)}) collective-permute-start(f32[2,16,128]{2,1,0:T(8,128)} %param.5), channel_id=1, source_target_pairs={{16,0},{32,16},{48,32},{64,48},{80,64},{96,80},{112,96},{128,112},... | collective-permute-start | bytes 49160 | tf_op jit(solution)/shard_map/ppermute | solution.py:114
  11.9 0.7 %fusion.3.mask_ref = f32[5]{0:T(128)S(1)} fusion(s32[2,5]{1,0:T(2,128)} %param.6, s32[]{:T(128)S(6)} %select_n.40), kind=kLoop, calls=%fused_computation.14 | loop fusion | flops 5 | bytes 44 | tf_op jit(solution)/shard_map/convert_element_type | solution.py:124
  13.2 4.4 %collective-permute-done = f32[2,16,128]{2,1,0:T(8,128)S(1)} collective-permute-done((f32[2,16,128]{2,1,0:T(8,128)}, f32[2,16,128]{2,1,0:T(8,128)S(1)}, u32[]{:S(2)}, u32[]{:S(2)}) %collective-permute-start) | collective-permute-done | bytes 16416 | tf_op jit(solution)/shard_map/ppermute | solution.py:113
  17.7 0.0 collective-permute-done.1
  17.7 0.7 %pad_maximum_fusion.1 = f32[6,16,128]{2,1,0:T(8,128)S(1)} fusion(f32[2,16,128]{2,1,0:T(8,128)S(1)} %collective-permute-done.1, f32[2,16,128]{2,1,0:T(8,128)} %param.5, f32[2,16,128]{2,1,0:T(8,128)S(1)} %collective-permute-done), kind=kLoop, calls=%fused_computation.10 | loop fusion | flops 24576 | bytes 98304 | tf_op jit(solution)/shard_map/concatenate | solution.py:115
  18.4 24.4 %all_gather.3 = f32[6,256,128]{2,1,0:T(8,128)S(1)} all-gather(f32[6,16,128]{2,1,0:T(8,128)S(1)} %pad_maximum_fusion.1), channel_id=1, replica_groups=mesh['cols'=32,'rep'=16] {'rep'}, dimensions={1}, use_global_device_ids=true | all-gather | bytes 835584 | tf_op jit(solution)/shard_map/all_gather | solution.py:121
  42.9 0.0 collective-permute-done.2
  42.9 0.0 collective-permute-done.3
  42.9 0.0 copy-done
  42.9 0.4 fusion.1.hb_ref
  43.3 11.6 %shard_map.46 = f32[80,640]{1,0:T(8,128)S(1)} custom-call(f32[5]{0:T(128)S(1)} %fusion.3.mask_ref, f32[1]{0:T(128)S(6)} %copy.5.fermi_ref, s32[1]{0:T(128)} %bitcast.1.row_ref, f32[5,256,128]{2,1,0:T(8,128)S(1)} %constant_dynamic-slice_fusion.y_ref, f32[5,5,128,128]{3,2,1,0:T(8,128)S(1)} %fusion.1.hb_ref), custom_call_target="tpu_custom_call" | custom-call | tf_op jit(solution)/shard_map/pallas_call | solution.py:100
  54.9 2.7 %collective-permute-start.4 = (f32[40,640]{1,0:T(8,128)S(1)}, f32[40,640]{1,0:T(8,128)S(1)}, u32[]{:S(2)}, u32[]{:S(2)}) collective-permute-start(f32[40,640]{1,0:T(8,128)S(1)} %slice_select_fusion), channel_id=1, source_target_pairs={{0,1},{1,0},{2,3},{3,2},{4,5},{5,4},{6,7},{7,6},{8,9},{9,8},{10,11... | collective-permute-start | bytes 307208 | tf_op jit(solution)/shard_map/ppermute | solution.py:131
  57.6 3.8 %collective-permute-done.4 = f32[40,640]{1,0:T(8,128)S(1)} collective-permute-done((f32[40,640]{1,0:T(8,128)S(1)}, f32[40,640]{1,0:T(8,128)S(1)}, u32[]{:S(2)}, u32[]{:S(2)}) %collective-permute-start.4) | collective-permute-done | bytes 102432 | tf_op jit(solution)/shard_map/ppermute | solution.py:131
  61.4 0.7 %pad_maximum_fusion = f32[2,40,640]{2,1,0:T(8,128)} fusion(f32[1,40,640]{2,1,0:T(8,128)S(1)} %get-tuple-element.6, f32[1,40,640]{2,1,0:T(8,128)S(1)} %get-tuple-element.5), kind=kLoop, calls=%fused_computation.5 | loop fusion | flops 51200 | bytes 409600 | tf_op jit(solution)/shard_map/stack | solution.py:132
  (3 shorter events, 0.1 us)
Async XLA Ops:
  0.0 42.9 %copy-start = (f32[2,5,128,128]{3,2,1,0:T(8,128)S(1)}, f32[2,5,128,128]{3,2,1,0:T(8,128)}, u32[]{:S(2)}) copy-start(f32[2,5,128,128]{3,2,1,0:T(8,128)} %param.4) | copy-start | bytes 1966084
  0.0 42.9 %collective-permute-start.2 = (f32[2,5,128,128]{3,2,1,0:T(8,128)}, f32[2,5,128,128]{3,2,1,0:T(8,128)S(1)}, u32[]{:S(2)}, u32[]{:S(2)}) collective-permute-start(f32[2,5,128,128]{3,2,1,0:T(8,128)} %param.4), channel_id=1, source_target_pairs={{0,16},{16,32},{32,48},{48,64},{64,80},{80,96},{96,112},{112,128},... | collective-permute-start | bytes 1966088 | tf_op jit(solution)/shard_map/ppermute | solution.py:113
  0.0 42.9 %collective-permute-start.3 = (f32[2,5,128,128]{3,2,1,0:T(8,128)}, f32[2,5,128,128]{3,2,1,0:T(8,128)S(1)}, u32[]{:S(2)}, u32[]{:S(2)}) collective-permute-start(f32[2,5,128,128]{3,2,1,0:T(8,128)} %param.4), channel_id=1, source_target_pairs={{16,0},{32,16},{48,32},{64,48},{80,64},{96,80},{112,96},{128,112},... | collective-permute-start | bytes 1966088 | tf_op jit(solution)/shard_map/ppermute | solution.py:114
  8.9 8.7 %collective-permute-start = (f32[2,16,128]{2,1,0:T(8,128)}, f32[2,16,128]{2,1,0:T(8,128)S(1)}, u32[]{:S(2)}, u32[]{:S(2)}) collective-permute-start(f32[2,16,128]{2,1,0:T(8,128)} %param.5), channel_id=1, source_target_pairs={{0,16},{16,32},{32,48},{48,64},{64,80},{80,96},{96,112},{112,128},... | collective-permute-start | bytes 49160 | tf_op jit(solution)/shard_map/ppermute | solution.py:113
  9.0 8.7 %collective-permute-start.1 = (f32[2,16,128]{2,1,0:T(8,128)}, f32[2,16,128]{2,1,0:T(8,128)S(1)}, u32[]{:S(2)}, u32[]{:S(2)}) collective-permute-start(f32[2,16,128]{2,1,0:T(8,128)} %param.5), channel_id=1, source_target_pairs={{16,0},{32,16},{48,32},{64,48},{80,64},{96,80},{112,96},{128,112},... | collective-permute-start | bytes 49160 | tf_op jit(solution)/shard_map/ppermute | solution.py:114
  54.9 6.6 %collective-permute-start.4 = (f32[40,640]{1,0:T(8,128)S(1)}, f32[40,640]{1,0:T(8,128)S(1)}, u32[]{:S(2)}, u32[]{:S(2)}) collective-permute-start(f32[40,640]{1,0:T(8,128)S(1)} %slice_select_fusion), channel_id=1, source_target_pairs={{0,1},{1,0},{2,3},{3,2},{4,5},{5,4},{6,7},{7,6},{8,9},{9,8},{10,11... | collective-permute-start | bytes 307208 | tf_op jit(solution)/shard_map/ppermute | solution.py:131

commit v2 on v1

v2 whole, which is shorter than its diff:
```python
import functools
import jax, jax.numpy as jnp
from jax import lax
from jax.experimental import pallas as pl
from jax.experimental.pallas import tpu as pltpu
from jax.sharding import PartitionSpec as P

B = 128
NC = 5
M = 640
PS = 256
ROWS = 80
PIECE = 40
SIDE = 4
F32 = jnp.float32
BF = jnp.bfloat16
MESH = pl.DeviceIdType.MESH


def split(x):
    hi = x.astype(BF)
    return hi, (x - hi.astype(F32)).astype(BF)


def dot(a, b):
    return jnp.dot(a, b, preferred_element_type=F32)


def dot_nt(a, b):
    return lax.dot_general(a, b, (((1,), (1,)), ((), ())), preferred_element_type=F32)


def dot3(a, b, d=dot):
    (ah, al), (bh, bl) = a, b
    return d(ah, bh) + d(ah, bl) + d(al, bh)


class Net:
    def __init__(self, send, recv):
        self.send, self.recv = send, recv
        self.slots = 0
        self.sent = []

    def slot(self):
        self.slots += 1
        return self.slots - 1

    def copy(self, slot, src, dst, dev):
        c = pltpu.make_async_remote_copy(
            src_ref=src, dst_ref=dst, send_sem=self.send.at[slot], recv_sem=self.recv.at[slot],
            device_id=dev, device_id_type=MESH)
        c.start()
        self.sent.append(c)

    def arrived(self, slot, dst, dev):
        pltpu.make_async_remote_copy(
            src_ref=dst, dst_ref=dst, send_sem=self.send.at[slot], recv_sem=self.recv.at[slot],
            device_id=dev, device_id_type=MESH).wait_recv()


SLOTS = 64


def gather(ncol, hb_ref, mf_ref, yb, hbuf, net, loc):
    c = lax.axis_index("cols")
    r = lax.axis_index("rep")
    y, x = r // SIDE, r % SIDE
    g = x % 2
    up, down = (c + 1) % ncol, (c + ncol - 1) % ncol
    xs = [x, (x + 3) % 4, (x + 1) % 4, (x + 2) % 4]
    ys = [y, (y + 3) % 4, (y + 1) % 4, (y + 2) % 4]
    dev_c = {+1: (up, r), -1: (down, r)}
    dev_x = {+1: (c, y * 4 + xs[2]), -1: (c, y * 4 + xs[1])}
    dev_y = {+1: (c, ys[2] * 4 + x), -1: (c, ys[1] * 4 + x)}
    barrier = pltpu.get_barrier_semaphore()
    for d in (dev_c, dev_x, dev_y):
        for s in (+1, -1):
            pl.semaphore_signal(barrier, inc=1, device_id=d[s], device_id_type=MESH)
    pl.semaphore_wait(barrier, 6)

    def at(h, w, p1, p2, n=None):
        ws = pl.ds(w, n) if n else slice(None)
        return yb.at[ws, h, p1, p2]

    first = {0: (xs, dev_x), 1: (ys, dev_y)}
    second = {0: (ys, dev_y), 1: (xs, dev_x)}
    cs = {(s, h): net.slot() for h in (0, 1) for s in (+1, -1)}
    for h in (0, 1):
        p1, p2 = second[h][0][0], first[h][0][0]
        for s, w in ((+1, 0), (-1, 4)):
            net.copy(cs[s, h], mf_ref.at[:, 8 * h:8 * h + 8], at(h, w, p1, p2, 2), dev_c[s])
    local = []
    for h in (0, 1):
        p1, p2 = second[h][0][0], first[h][0][0]
        l = pltpu.make_async_copy(mf_ref.at[:, 8 * h:8 * h + 8], at(h, 2, p1, p2, 2), loc.at[h])
        l.start()
        local.append(l)
    hs = [net.slot() for _ in range(3)]
    plans = {
        0: ([(+1, 1, 1, 1, 5), (+1, 0, 0, 2, 5), (-1, 0, 4, 0, 3)], [(0, 2, 0, 5), (1, 3, 0, 4)]),
        1: ([(-1, 0, 3, 0, 4), (-1, 1, 4, 0, 3), (+1, 1, 0, 2, 5)], [(1, 2, 0, 5), (0, 1, 1, 5)]),
    }
    for gg in (0, 1):
        @pl.when(g == gg)
        def _():
            for slot, (s, k, a, e0, e1) in zip(hs, plans[gg][0]):
                pltpu.make_async_remote_copy(
                    src_ref=hb_ref.at[k, e0:e1], dst_ref=hbuf.at[a, e0:e1], send_sem=net.send.at[slot],
                    recv_sem=net.recv.at[slot], device_id=dev_c[s], device_id_type=MESH).start()
            for i, (k, a, e0, e1) in enumerate(plans[gg][1]):
                pltpu.make_async_copy(hb_ref.at[k, e0:e1], hbuf.at[a, e0:e1], loc.at[2 + i]).start()

    s1 = {(h, s): net.slot() for h in (0, 1) for s in (+1, -1)}
    s1r = {(h, s): net.slot() for h in (0, 1) for s in (+1, -1)}
    s2 = {(h, p, s): net.slot() for h in (0, 1) for p in range(4) for s in (+1, -1)}
    s2r = {(h, p, s): net.slot() for h in (0, 1) for p in range(4) for s in (+1, -1)}

    def span2(h):
        return (g, 5) if h == 0 else (0, 6)

    def parts2(h):
        return ((g, 3), (g + 3, 2)) if h == 0 else ((0, 3), (3, 3))

    def send2(h, p):
        qs, dev = second[h]
        pos = first[h][0][p]
        w, n = span2(h)
        for s in (+1, -1):
            ref = at(h, w, qs[0], pos, n)
            net.copy(s2[h, p, s], ref, ref, dev[s])

    def relay2(h, p):
        qs, dev = second[h]
        pos = first[h][0][p]
        w, n = span2(h)
        for s, q, (w0, n0) in ((+1, qs[1], parts2(h)[0]), (-1, qs[2], parts2(h)[1])):
            net.arrived(s2[h, p, s], at(h, w, q, pos, n), dev[-s])
            ref = at(h, w0, q, pos, n0)
            net.copy(s2r[h, p, s], ref, ref, dev[s])

    for h in (0, 1):
        qs, ps = second[h][0], first[h][0]
        local[h].wait()
        for s, w in ((+1, 0), (-1, 4)):
            net.arrived(cs[s, h], at(h, w, qs[0], ps[0], 2), dev_c[-s])
        for s in (+1, -1):
            ref = at(h, 0, qs[0], ps[0], 6)
            net.copy(s1[h, s], ref, ref, first[h][1][s])
    for h in (0, 1):
        send2(h, 0)
    for h in (0, 1):
        qs, (ps, dev) = second[h][0], first[h]
        for s, p, w in ((+1, 1, 0), (-1, 2, 3)):
            net.arrived(s1[h, s], at(h, 0, qs[0], ps[p], 6), dev[-s])
            ref = at(h, w, qs[0], ps[p], 3)
            net.copy(s1r[h, s], ref, ref, dev[s])
    for h in (0, 1):
        send2(h, 1)
        send2(h, 2)
    for h in (0, 1):
        relay2(h, 0)
    for h in (0, 1):
        qs, (ps, dev) = second[h][0], first[h]
        for s, w in ((+1, 0), (-1, 3)):
            net.arrived(s1r[h, s], at(h, w, qs[0], ps[3], 3), dev[-s])
        send2(h, 3)
    for p in (1, 2, 3):
        for h in (0, 1):
            relay2(h, p)
    for gg in (0, 1):
        @pl.when(g == gg)
        def _():
            for slot, (s, k, a, e0, e1) in zip(hs, plans[gg][0]):
                d = pltpu.make_async_remote_copy(
                    src_ref=hb_ref.at[k, e0:e1], dst_ref=hbuf.at[a, e0:e1], send_sem=net.send.at[slot],
                    recv_sem=net.recv.at[slot], device_id=dev_c[s], device_id_type=MESH)
                d.wait()
            for i, (k, a, e0, e1) in enumerate(plans[gg][1]):
                pltpu.make_async_copy(hb_ref.at[k, e0:e1], hbuf.at[a, e0:e1], loc.at[2 + i]).wait()
    for p in range(4):
        for h in (0, 1):
            qs, dev = second[h]
            for s, (w0, n0) in ((+1, parts2(h)[0]), (-1, parts2(h)[1])):
                net.arrived(s2r[h, p, s], at(h, w0, qs[3], first[h][0][p], n0), dev[-s])


def fused(ncol, mask_ref, fermi_ref, hb_ref, mf_ref, out_ref, yb, hbuf, h_ref, yt_ref, x_ref, lw_ref, rw_ref,
          stage, send, recv, loc):
    c = lax.axis_index("cols")
    r = lax.axis_index("rep")
    g = r % 2
    net = Net(send, recv)
    gather(ncol, hb_ref, mf_ref, yb, hbuf, net, loc)
    mask = [mask_ref[g, a].astype(F32) for a in range(NC)]
    ys = [yb[g + a].reshape(PS, B) * mask[a] for a in range(NC)]
    for a in range(NC):
        yt_ref[a * B:(a + 1) * B, :] = ys[a].T
    yt = split(yt_ref[...])
    y = split(jnp.concatenate(ys, axis=1))
    for a in range(NC):
        for b in range(NC):
            sl = (slice(a * B, (a + 1) * B), slice(b * B, (b + 1) * B))
            if abs(a - b) <= 2:
                w = 0.5 * mask[a] * mask[b]
                h_ref[sl] = (hbuf[b, a - b + 2] + hbuf[a, b - a + 2].T) * w
            else:
                h_ref[sl] = jnp.zeros((B, B), F32)
    eye = lax.broadcasted_iota(jnp.int32, (PS, PS), 0) == lax.broadcasted_iota(jnp.int32, (PS, PS), 1)
    k = dot3(y, yt)
    one = jnp.ones((1, 1), F32)
    sumsq = M * one + 2.0 * jnp.sum(jnp.where(eye, k, 0.0), keepdims=True) + jnp.sum(k * k, keepdims=True)
    cs = 2.0 * jnp.sqrt(sumsq / M)
    al = 1.0 / cs
    t = 0.5 * (3.0 - al)
    u = 0.5 * (3.0 - al * t * t)
    ks = split(k)
    k2 = dot3(ks, ks)
    b0 = al * t * (t - al)
    b1 = al * al * (0.25 * al - t)
    b2 = 0.25 * al * al * al
    bm = b1 * k + b2 * k2 + jnp.where(eye, b0, 0.0)
    kb = dot3(ks, split(bm))
    rs = lax.rsqrt(cs)
    rm = (-0.5 * t * bm + 0.25 * al * kb - jnp.where(eye, 0.5 * al * u, 0.0)) * rs
    a0 = t * u * rs
    vts = split(dot3(yt, split(rm)))
    pt = dot3(split(h_ref[...]), yt)
    n = dot3(y, split(pt))
    pt2 = a0 * pt + 0.5 * dot3(vts, split(n))
    x_ref[...] = dot3(split(pt2), vts, dot_nt)
    mu = fermi_ref[0]
    a2 = a0 * a0
    acc = jnp.zeros((1, 1), F32)
    for a in range(NC):
        for b in range(NC):
            sl = (slice(a * B, (a + 1) * B), slice(b * B, (b + 1) * B))
            e = x_ref[sl] + x_ref[sl[1], sl[0]].T
            if abs(a - b) <= 2:
                e = e + a2 * h_ref[sl]
            if a == b:
                ey = lax.broadcasted_iota(jnp.int32, (B, B), 0) == lax.broadcasted_iota(jnp.int32, (B, B), 1)
                e = e - jnp.where(ey, mu, 0.0)
            acc = acc + jnp.sum(e * e, keepdims=True)
            h_ref[sl] = e
    inv = 1.0 / (2.0 * jnp.sqrt(acc / M + 1e-5))
    x0 = h_ref[...] * inv
    xh, xl = split(x0)
    lw_ref[:, 0:M] = xh
    lw_ref[:, M:2 * M] = xl
    lw_ref[:, 2 * M:3 * M] = xh
    rw_ref[0:M, :] = xh
    rw_ref[M:2 * M, :] = xh
    rw_ref[2 * M:3 * M, :] = xl
    ah, alo = split(dot(lw_ref[...], rw_ref[...]))
    rw_ref[0:M, :] = ah
    rw_ref[M:2 * M, :] = ah
    rw_ref[2 * M:3 * M, :] = alo
    x1 = 1.5 * x0 - 0.5 * dot(lw_ref[...], rw_ref[...])
    x_ref[...] = x1
    xh, xl = split(x1)
    rw_ref[0:M, :] = xh
    rw_ref[M:2 * M, :] = xh
    rw_ref[2 * M:3 * M, :] = xl
    r0 = pl.multiple_of((r // 2) * ROWS, 8)
    xr = x_ref[pl.ds(r0, ROWS), :]
    rh, rl = split(xr)
    q = dot(jnp.concatenate([rh, rl, rh], axis=1), rw_ref[...])
    qh, ql = split(q)
    cube = dot(jnp.concatenate([qh, ql, qh], axis=1), rw_ref[...])
    x2 = 1.5 * xr - 0.5 * cube
    ii = lax.broadcasted_iota(jnp.int32, (ROWS, M), 0) + r0
    jj = lax.broadcasted_iota(jnp.int32, (ROWS, M), 1)
    stage[...] = jnp.where(ii == jj, 0.5, 0.0) - 0.5 * x2
    partner = (c, r + 1 - 2 * g)
    fs = net.slot()
    theirs = stage.at[pl.ds(pl.multiple_of(PIECE * (1 - g), 8), PIECE)]
    net.copy(fs, theirs, out_ref.at[g], partner)
    out_ref[g] = stage[pl.ds(pl.multiple_of(PIECE * g, 8), PIECE)]
    for s in net.sent:
        s.wait_send()
    net.arrived(fs, out_ref.at[1 - g], partner)
    assert net.slots <= SLOTS


def on_device(ncol, hamiltonian_band, margin_factors, neighbour_mask, fermi_level):
    vm = pl.BlockSpec(memory_space=pltpu.VMEM)
    sm = pl.BlockSpec(memory_space=pltpu.SMEM)
    return pl.pallas_call(
        functools.partial(fused, ncol),
        out_shape=jax.ShapeDtypeStruct((2, PIECE, M), F32),
        in_specs=[sm, sm, pl.BlockSpec(memory_space=pl.ANY), vm],
        out_specs=vm,
        scratch_shapes=[
            pltpu.VMEM((6, 2, 4, 4, 8, B), F32),
            pltpu.VMEM((NC, NC, B, B), F32),
            pltpu.VMEM((M, M), F32),
            pltpu.VMEM((M, PS), F32),
            pltpu.VMEM((M, M), F32),
            pltpu.VMEM((M, 3 * M), BF),
            pltpu.VMEM((3 * M, M), BF),
            pltpu.VMEM((ROWS, M), F32),
            pltpu.SemaphoreType.DMA((SLOTS,)),
            pltpu.SemaphoreType.DMA((SLOTS,)),
            pltpu.SemaphoreType.DMA((4,)),
        ],
        compiler_params=pltpu.CompilerParams(collective_id=0, has_side_effects=True, vmem_limit_bytes=50 << 20),
    )(neighbour_mask, fermi_level, hamiltonian_band, margin_factors)


def solution(mesh):
    in_specs = (P("cols", None, None, None), P("cols", "rep", None), P("cols", None), P())
    return jax.shard_map(
        functools.partial(on_device, mesh.shape["cols"]), mesh=mesh, in_specs=in_specs,
        out_specs=P("cols", "rep", None), check_vma=False)
```

time: 62.4 us -> 47.2 us (0.76)
  the two profiles are of different devices: /device:TPU:2 before, /device:TPU:4 now
where the time goes in v2:
time: 47.2 us; the launch traced here: 47 us
  Pallas kernels  43.8 us (93%)
  local copies, waits for them, and re-layouts  2.49 us (5%)
  between operations  0.68 us (1%)
    pallas_call x1, Pallas kernels, on_device(): pl.pallas_call(functools.partial(fused, ncol), out_shape=jax.ShapeDtypeSt...  43.8 us
    unnamed x7, local copies, waits for them, and re-layouts  2.49 us

profile of v2, /device:TPU:4, one launch (start us, length us, event | category | flops | bytes accessed | tf_op | source)
XLA Modules:
  0.0 47.0 jit_solution(17466493282013486426)
XLA Ops:
  0.0 0.0 copy-start.2
  0.7 0.0 copy-done.2
  0.7 0.0 copy-start
  0.7 1.1 %copy-done = f32[2,5,128,128]{3,2,1,0:T(8,128)S(1)} copy-done((f32[2,5,128,128]{3,2,1,0:T(8,128)S(1)}, f32[2,5,128,128]{3,2,1,0:T(8,128)}, u32[]{:S(2)}) %copy-start) | copy-done | bytes 655384
  1.8 0.0 copy-start.1
  1.8 0.7 %copy-done.1 = f32[2,16,128]{2,1,0:T(8,128)S(1)} copy-done((f32[2,16,128]{2,1,0:T(8,128)S(1)}, f32[2,16,128]{2,1,0:T(8,128)}, u32[]{:S(2)}) %copy-start.1) | copy-done | bytes 16408
  2.5 43.8 %shard_map.46 = f32[2,40,640]{2,1,0:T(8,128)S(1)} custom-call(s32[2,5]{1,0:T(2,128)S(1)} %copy-done.2, f32[1]{0:T(128)S(6)} %copy.6.fermi_ref, f32[2,5,128,128]{3,2,1,0:T(8,128)S(1)} %copy-done, f32[2,16,128]{2,1,0:T(8,128)S(1)} %copy-done.1), custom_call_target="tpu_custom_call" | custom-call | tf_op jit(solution)/shard_map/pallas_call | solution.py:288
  46.3 0.7 %copy.7 = f32[2,40,640]{2,1,0:T(8,128)} copy(f32[2,40,640]{2,1,0:T(8,128)S(1)} %shard_map.46) | data formatting | bytes 409600
Async XLA Ops:
  0.0 0.7 %copy-start.2 = (s32[2,5]{1,0:T(2,128)S(1)}, s32[2,5]{1,0:T(2,128)}, u32[]{:S(2)}) copy-start(s32[2,5]{1,0:T(2,128)} %mask_ref.1) | copy-start | bytes 124
  0.7 1.1 %copy-start = (f32[2,5,128,128]{3,2,1,0:T(8,128)S(1)}, f32[2,5,128,128]{3,2,1,0:T(8,128)}, u32[]{:S(2)}) copy-start(f32[2,5,128,128]{3,2,1,0:T(8,128)} %hb_ref.1) | copy-start | bytes 1966084
  1.8 0.7 %copy-start.1 = (f32[2,16,128]{2,1,0:T(8,128)S(1)}, f32[2,16,128]{2,1,0:T(8,128)}, u32[]{:S(2)}) copy-start(f32[2,16,128]{2,1,0:T(8,128)} %mf_ref.1) | copy-start | bytes 49156

commit v3 on v1

v3 whole, which is shorter than its diff:
```python
import functools
import jax, jax.numpy as jnp
from jax import lax
from jax.experimental import pallas as pl
from jax.experimental.pallas import tpu as pltpu
from jax.sharding import PartitionSpec as P

B = 128
NC = 5
M = 640
PS = 256
ROWS = 80
PIECE = 40
SIDE = 4
F32 = jnp.float32
BF = jnp.bfloat16
MESH = pl.DeviceIdType.MESH


def split(x):
    hi = x.astype(BF)
    return hi, (x - hi.astype(F32)).astype(BF)


def dot(a, b):
    return jnp.dot(a, b, preferred_element_type=F32)


def dot_nt(a, b):
    return lax.dot_general(a, b, (((1,), (1,)), ((), ())), preferred_element_type=F32)


def dot3(a, b, d=dot):
    (ah, al), (bh, bl) = a, b
    return d(ah, bh) + d(ah, bl) + d(al, bh)


class Net:
    def __init__(self, send, recv):
        self.send, self.recv = send, recv
        self.slots = 0
        self.sent = []

    def slot(self):
        self.slots += 1
        return self.slots - 1

    def copy(self, slot, src, dst, dev):
        c = pltpu.make_async_remote_copy(
            src_ref=src, dst_ref=dst, send_sem=self.send.at[slot], recv_sem=self.recv.at[slot],
            device_id=dev, device_id_type=MESH)
        c.start()
        self.sent.append(c)

    def arrived(self, slot, dst, dev):
        pltpu.make_async_remote_copy(
            src_ref=dst, dst_ref=dst, send_sem=self.send.at[slot], recv_sem=self.recv.at[slot],
            device_id=dev, device_id_type=MESH).wait_recv()


SLOTS = 96
TILES = ((0, 256), (256, 512), (512, 640))
BLOCKS = {
    0: {+1: ((1, 1, 1, 5), (0, 0, 2, 5)), -1: ((0, 4, 0, 3),)},
    1: {+1: ((1, 0, 2, 5),), -1: ((0, 3, 0, 4), (1, 4, 0, 3))},
}
OWN = {0: ((0, 2, 0, 5), (1, 3, 0, 4)), 1: ((1, 2, 0, 5), (0, 1, 1, 5))}
OFFSETS = (0, 1, 3, 2)


def gather(ncol, c, r, g, gd, hb_ref, mf_ref, yb, hbuf, net, loc):
    y, x = r // SIDE, r % SIDE
    up, down = (c + 1) % ncol, (c + ncol - 1) % ncol
    cols = {0: c, +1: up, -1: down}

    def dev(dc, h, dp):
        if h == 0:
            return (cols[dc], y * SIDE + (x + dp) % SIDE)
        return (cols[dc], ((y + dp) % SIDE) * SIDE + x)

    barrier = pltpu.get_barrier_semaphore()
    partners = [dev(dc, h, dp) for h in (0, 1) for dp in OFFSETS for dc in (0, +1, -1)
                if not (dp == 0 and (dc == 0 or h == 1))]
    for d in partners:
        pl.semaphore_signal(barrier, inc=1, device_id=d, device_id_type=MESH)
    pl.semaphore_wait(barrier, len(partners))

    mine = {0: x, 1: y}

    def at(h, w, n, second, first):
        return yb.at[pl.ds(w, n), h, second, first]

    group = {0: 2, +1: 0, -1: 4}
    s1 = {(h, dc, dp): net.slot() for h in (0, 1) for dc in (0, +1, -1) for dp in OFFSETS if (dc, dp) != (0, 0)}
    order = ([(h, dc, 0) for h in (0, 1) for dc in (+1, -1)]
             + [(h, dc, dp) for dp in (2, 1, 3) for h in (0, 1) for dc in (+1, -1, 0)])
    for h, dc, dp in order:
        net.copy(s1[h, dc, dp], mf_ref.at[:, 8 * h:8 * h + 8], at(h, group[dc], 2, mine[1 - h], mine[h]), dev(dc, h, dp))
    local = []
    for h in (0, 1):
        l = pltpu.make_async_copy(mf_ref.at[:, 8 * h:8 * h + 8], at(h, 2, 2, mine[1 - h], mine[h]), loc.at[h])
        l.start()
        local.append(l)
    hs = {(s, i): net.slot() for s in (+1, -1) for i in (0, 1)}

    def blocks(s, i, k, a, e0, e1):
        return pltpu.make_async_remote_copy(
            src_ref=hb_ref.at[k, e0:e1], dst_ref=hbuf.at[a, e0:e1], send_sem=net.send.at[hs[s, i]],
            recv_sem=net.recv.at[hs[s, i]], device_id=dev(s, 0, 0), device_id_type=MESH)

    for gg in (0, 1):
        @pl.when(gd == gg)
        def _():
            for s in (+1, -1):
                for i, b in enumerate(BLOCKS[gg][s]):
                    blocks(s, i, *b).start()

        @pl.when(g == gg)
        def _():
            for i, (k, a, e0, e1) in enumerate(OWN[gg]):
                pltpu.make_async_copy(hb_ref.at[k, e0:e1], hbuf.at[a, e0:e1], loc.at[2 + i]).start()

    s2 = {(h, dp, s): net.slot() for h in (0, 1) for dp in OFFSETS for s in (+1, -1)}
    s2r = {(h, dp, s): net.slot() for h in (0, 1) for dp in OFFSETS for s in (+1, -1)}
    halves = {+1: (0, 3), -1: (3, 3)}

    def place(h, dp):
        return (mine[h] + 4 - dp) % SIDE

    def along(h, s):
        return dev(0, 1 - h, s)

    def second(h, s):
        return (mine[1 - h] + 4 + s) % SIDE

    for dp in OFFSETS:
        for h in (0, 1):
            if dp == 0:
                local[h].wait()
            for dc in (0, +1, -1):
                if (dc, dp) != (0, 0):
                    net.arrived(s1[h, dc, dp], at(h, group[dc], 2, mine[1 - h], place(h, dp)), dev(0, h, dp))
            ref = at(h, 0, 6, mine[1 - h], place(h, dp))
            for s in (+1, -1):
                net.copy(s2[h, dp, s], ref, ref, along(h, s))
    for dp in OFFSETS:
        for h in (0, 1):
            for s in (+1, -1):
                net.arrived(s2[h, dp, s], at(h, 0, 6, second(h, -s), place(h, dp)), along(h, -s))
                ref = at(h, *halves[s], second(h, -s), place(h, dp))
                net.copy(s2r[h, dp, s], ref, ref, along(h, s))
    for gg in (0, 1):
        @pl.when(g == gg)
        def _():
            for s in (+1, -1):
                for i, b in enumerate(BLOCKS[gg][s]):
                    blocks(s, i, *b).wait_recv()
            for i, (k, a, e0, e1) in enumerate(OWN[gg]):
                pltpu.make_async_copy(hb_ref.at[k, e0:e1], hbuf.at[a, e0:e1], loc.at[2 + i]).wait()
    for dp in OFFSETS:
        for h in (0, 1):
            for s in (+1, -1):
                net.arrived(s2r[h, dp, s], at(h, *halves[s], second(h, 2), place(h, dp)), along(h, -s))

    def finish():
        for gg in (0, 1):
            @pl.when(gd == gg)
            def _():
                for s in (+1, -1):
                    for i, b in enumerate(BLOCKS[gg][s]):
                        blocks(s, i, *b).wait_send()
    return finish


def cat3l(a, b):
    return jnp.concatenate([a, b, a], axis=1)


def cdot(a, b):
    return dot(cat3l(*a), jnp.concatenate([b[0], b[0], b[1]], axis=0))


def fused(ncol, mask_hbm, fermi_hbm, hb_ref, mf_ref, out_ref, yb, hbuf, h_ref, yt_ref, x_ref, eh_ref, el_ref,
          stage, mask_ref, fermi_ref, send, recv, loc):
    c = lax.axis_index("cols")
    r = lax.axis_index("rep")
    y, x = r // SIDE, r % SIDE
    core = c % 2
    g = (x * (1 - core) + y * core) % 2
    gd = (x * core + y * (1 - core)) % 2
    other = r + (1 - 2 * g) * (1 + 3 * core)
    small = [pltpu.make_async_copy(mask_hbm, mask_ref, loc.at[4]), pltpu.make_async_copy(fermi_hbm, fermi_ref, loc.at[5])]
    for s in small:
        s.start()
    net = Net(send, recv)
    finish = gather(ncol, c, r, g, gd, hb_ref, mf_ref, yb, hbuf, net, loc)
    for s in small:
        s.wait()
    mask = [mask_ref[g, a].astype(F32) for a in range(NC)]
    mu = fermi_ref[0]
    ys = [yb[g + a].reshape(PS, B) * mask[a] for a in range(NC)]
    for a in range(NC):
        yt_ref[a * B:(a + 1) * B, :] = ys[a].T
    yt = split(yt_ref[...])
    yy = split(jnp.concatenate(ys, axis=1))
    for a in range(NC):
        for b in range(NC):
            sl = (slice(a * B, (a + 1) * B), slice(b * B, (b + 1) * B))
            if abs(a - b) <= 2:
                w = 0.5 * mask[a] * mask[b]
                h_ref[sl] = (hbuf[b, a - b + 2] + hbuf[a, b - a + 2].T) * w
            else:
                h_ref[sl] = jnp.zeros((B, B), F32)
    eye = lax.broadcasted_iota(jnp.int32, (PS, PS), 0) == lax.broadcasted_iota(jnp.int32, (PS, PS), 1)
    k = cdot(yy, yt)
    ks = split(k)
    k2 = cdot(ks, ks)
    k3 = cdot(ks, split(k2))
    pt = cdot(split(h_ref[...]), yt)
    n = cdot(yy, split(pt))
    one = jnp.ones((1, 1), F32)
    sumsq = M * one + 2.0 * jnp.sum(jnp.where(eye, k, 0.0), keepdims=True) + jnp.sum(k * k, keepdims=True)
    cs = 2.0 * jnp.sqrt(sumsq / M)
    al = 1.0 / cs
    t = 0.5 * (3.0 - al)
    u = 0.5 * (3.0 - al * t * t)
    b0 = al * t * (t - al)
    b1 = al * al * (0.25 * al - t)
    b2 = 0.25 * al * al * al
    rs = lax.rsqrt(cs)
    q0 = (-0.5 * t * b0 - 0.5 * al * u) * rs
    q1 = (-0.5 * t * b1 + 0.25 * al * b0) * rs
    q2 = (-0.5 * t * b2 + 0.25 * al * b1) * rs
    q3 = (0.25 * al * b2) * rs
    a0 = t * u * rs
    rm = q1 * k + q2 * k2 + q3 * k3 + jnp.where(eye, q0, 0.0)
    vts = split(cdot(yt, split(rm)))
    pts = split(a0 * pt + 0.5 * cdot(vts, split(n)))
    a2 = a0 * a0
    lh, ll = (jnp.concatenate([pts[i], vts[i]], axis=1) for i in (0, 1))
    rh, rl = (jnp.concatenate([vts[i], pts[i]], axis=1) for i in (0, 1))
    lcat = cat3l(lh, ll)
    rcat = jnp.concatenate([rh, rh, rl], axis=1)
    acc = jnp.zeros((1, 1), F32)
    for c0, c1 in TILES:
        e = dot_nt(lcat, rcat[c0:c1]) + a2 * h_ref[:, c0:c1]
        ii = lax.broadcasted_iota(jnp.int32, e.shape, 0)
        jj = lax.broadcasted_iota(jnp.int32, e.shape, 1) + c0
        e = e - jnp.where(ii == jj, mu, 0.0)
        acc = acc + jnp.sum(e * e, keepdims=True)
        eh_ref[:, c0:c1], el_ref[:, c0:c1] = split(e)
        x_ref[:, c0:c1] = e
    inv = 1.0 / (2.0 * jnp.sqrt(acc / M + 1e-5))

    def times(v, c0=0, c1=M):
        hi, lo = split(v)
        p = dot(jnp.concatenate([hi, lo], axis=0), eh_ref[:, c0:c1])
        return (p[:ROWS] + p[ROWS:] + dot(hi, el_ref[:, c0:c1])) * inv

    mine = pl.multiple_of(r * PIECE, 8)
    theirs = pl.multiple_of(other * PIECE, 8)
    x0 = jnp.concatenate([x_ref[pl.ds(mine, PIECE)], x_ref[pl.ds(theirs, PIECE)]], axis=0) * inv
    x1 = 1.5 * x0 - 0.5 * times(times(x0))
    p = times(x1)
    q = 1.5 * p - 0.5 * times(times(p))
    p = times(q)
    p2 = times(p)
    partner = (c, other)
    fs = [net.slot() for _ in TILES]
    for slot, (c0, c1) in zip(fs, TILES):
        x2 = 1.5 * x1[:, c0:c1] - 0.5 * (1.5 * p[:, c0:c1] - 0.5 * times(p2, c0, c1))
        ii = lax.broadcasted_iota(jnp.int32, (PIECE, c1 - c0), 0)
        jj = lax.broadcasted_iota(jnp.int32, (PIECE, c1 - c0), 1) + c0
        stage[:, c0:c1] = jnp.where(ii + theirs == jj, 0.5, 0.0) - 0.5 * x2[PIECE:]
        net.copy(slot, stage.at[:, c0:c1], out_ref.at[g, :, c0:c1], partner)
        out_ref[g, :, c0:c1] = jnp.where(ii + mine == jj, 0.5, 0.0) - 0.5 * x2[:PIECE]
    for s in net.sent:
        s.wait_send()
    finish()
    for slot, (c0, c1) in zip(fs, TILES):
        net.arrived(slot, out_ref.at[1 - g, :, c0:c1], partner)
    assert net.slots <= SLOTS


def on_device(ncol, hamiltonian_band, margin_factors, neighbour_mask, fermi_level):
    vm = pl.BlockSpec(memory_space=pltpu.VMEM)
    return pl.pallas_call(
        functools.partial(fused, ncol),
        out_shape=jax.ShapeDtypeStruct((2, PIECE, M), F32),
        in_specs=[pl.BlockSpec(memory_space=pltpu.HBM)] * 4,
        out_specs=vm,
        scratch_shapes=[
            pltpu.VMEM((6, 2, 4, 4, 8, B), F32),
            pltpu.VMEM((NC, NC, B, B), F32),
            pltpu.VMEM((M, M), F32),
            pltpu.VMEM((M, PS), F32),
            pltpu.VMEM((M, M), F32),
            pltpu.VMEM((M, M), BF),
            pltpu.VMEM((M, M), BF),
            pltpu.VMEM((PIECE, M), F32),
            pltpu.SMEM((2, NC), jnp.int32),
            pltpu.SMEM((1,), F32),
            pltpu.SemaphoreType.DMA((SLOTS,)),
            pltpu.SemaphoreType.DMA((SLOTS,)),
            pltpu.SemaphoreType.DMA((6,)),
        ],
        compiler_params=pltpu.CompilerParams(collective_id=0, has_side_effects=True, vmem_limit_bytes=63 << 20),
    )(neighbour_mask, fermi_level, hamiltonian_band, margin_factors)


def solution(mesh):
    in_specs = (P("cols", None, None, None), P("cols", "rep", None), P("cols", None), P())
    return jax.shard_map(
        functools.partial(on_device, mesh.shape["cols"]), mesh=mesh, in_specs=in_specs,
        out_specs=P("cols", "rep", None), check_vma=False)
```

time: 62.4 us -> 42.8 us (0.69)
  Pallas kernels: 11.6 us -> 40.3 us
  blocking collectives: 24.4 us -> 0 us
  starting transfers between devices: 14.6 us -> 0 us
  waiting for transfers between devices: 8.27 us -> 0 us
  other arithmetic: 2.51 us -> 0 us
  local copies, waits for them, and re-layouts: 0.05 us -> 1.62 us
    pallas_call x1, Pallas kernels: 11.6 us -> 40.3 us  [on_device(): pl.pallas_call(functools.partial(fused, ncol), out_shape=jax.ShapeDtypeSt...]
    all_gather x1 -> x0, blocking collectives: 24.4 us -> none  [on_device(): y = lax.all_gather(wide, 'rep', axis=1, tiled=True)]
    ppermute x5 -> x0, starting transfers between devices: 14.6 us -> none  [the longest x2 11.9 us: extended(): high = lax.ppermute(block, axis, bwd)]
    ppermute x5 -> x0, waiting for transfers between devices: 8.27 us -> none  [the longest x2 4.42 us: extended(): low = lax.ppermute(block, axis, fwd)]
    unnamed x2 -> x1, local copies, waits for them, and re-layouts: 0.01 us -> 1.62 us
    concatenate x2 -> x0, other arithmetic: 1.08 us -> none  [extended(): return jnp.concatenate([low, block, high], axis=0)]
    another operation x2 -> x0, other arithmetic: 0.73 us -> none  [on_device(): jnp.stack([jnp.where(g == 0, keep, got), jnp.where(g == 0, got, keep)])]
    convert_element_type x1 -> x0, other arithmetic: 0.68 us -> none  [on_device(): mask = lax.dynamic_slice_in_dim(neighbour_mask, g, 1, 0)[0].astype(F32)]
  transfers between devices with their start and end apart: 5 -> 0, of which waited for: 2 -> 0; matrix products, arithmetic and copies ran while one was open for 2% -> 0% of each run, Pallas kernels for 0% -> 0%
where the time goes in v3:
time: 42.8 us; the launch traced here: 42.6 us
  Pallas kernels  40.3 us (94%)
  local copies, waits for them, and re-layouts  1.62 us (4%)
  between operations  0.66 us (2%)
    pallas_call x1, Pallas kernels, on_device(): pl.pallas_call(functools.partial(fused, ncol), out_shape=jax.ShapeDtypeSt...  40.3 us
    unnamed x1, local copies, waits for them, and re-layouts  1.62 us

profile of v3, /device:TPU:2, one launch (start us, length us, event | category | flops | bytes accessed | tf_op | source)
XLA Modules:
  0.0 42.6 jit_solution(14371043442766403647)
XLA Ops:
  0.7 40.3 %shard_map.46 = f32[2,40,640]{2,1,0:T(8,128)} custom-call(s32[2,5]{1,0:T(2,128)} %mask_hbm.1, f32[1]{0:T(128)S(6)} %copy.6.fermi_hbm, f32[2,5,128,128]{3,2,1,0:T(8,128)} %hb_ref.1, f32[2,16,128]{2,1,0:T(8,128)} %mf_ref.1), custom_call_target="tpu_custom_call" | custom-call | tf_op jit(solution)/shard_map/pallas_call | solution.py:287
  41.0 1.6 %copy.7 = f32[2,40,640]{2,1,0:T(8,128)} copy(f32[2,40,640]{2,1,0:T(8,128)} %shard_map.46) | data formatting | bytes 409600

commit v4 on v3

--- a/solution.py
+++ b/solution.py
@@ -58,7 +58,7 @@
             device_id=dev, device_id_type=MESH).wait_recv()
 
 
-SLOTS = 96
+SLOTS = 64
 TILES = ((0, 256), (256, 512), (512, 640))
 BLOCKS = {
     0: {+1: ((1, 1, 1, 5), (0, 0, 2, 5)), -1: ((0, 4, 0, 3),)},
@@ -68,50 +68,91 @@
 OFFSETS = (0, 1, 3, 2)
 
 
-def gather(ncol, c, r, g, gd, hb_ref, mf_ref, yb, hbuf, net, loc):
-    y, x = r // SIDE, r % SIDE
-    up, down = (c + 1) % ncol, (c + ncol - 1) % ncol
-    cols = {0: c, +1: up, -1: down}
-
-    def dev(dc, h, dp):
+def gather(ncol, c, r, g, gd, hb_ref, mf_ref, yb, hbuf, net, loc, far_sem, between):
+    y, x = lax.div(r, SIDE), lax.rem(r, SIDE)
+    core = lax.rem(c, 2)
+    mate = c + 1 - 2 * core
+    far = lax.rem(c + ncol - 1 + 2 * core, ncol)
+
+    def dev(col, h, dp):
         if h == 0:
-            return (cols[dc], y * SIDE + (x + dp) % SIDE)
-        return (cols[dc], ((y + dp) % SIDE) * SIDE + x)
+            return (col, y * SIDE + (lax.rem(x + dp + 4, SIDE) if dp else x))
+        return (col, (lax.rem(y + dp + 4, SIDE) if dp else y) * SIDE + x)
+
+    def cross(col):
+        return [dev(col, h, dp) for h in (0, 1) for dp in OFFSETS if not (dp == 0 and h == 1)]
+
+    def greet(sem, d):
+        pl.semaphore_signal(sem, inc=1, device_id=d, device_id_type=MESH)
 
     barrier = pltpu.get_barrier_semaphore()
-    partners = [dev(dc, h, dp) for h in (0, 1) for dp in OFFSETS for dc in (0, +1, -1)
-                if not (dp == 0 and (dc == 0 or h == 1))]
-    for d in partners:
-        pl.semaphore_signal(barrier, inc=1, device_id=d, device_id_type=MESH)
-    pl.semaphore_wait(barrier, len(partners))
+    near = cross(c)[1:] + cross(mate)
+    for d in near:
+        greet(barrier, d)
+
+    @pl.when(core == 0)
+    def _():
+        for d in cross(far):
+            greet(barrier, d)
+    pl.semaphore_wait(barrier, len(near) + 7 * core)
 
     mine = {0: x, 1: y}
 
     def at(h, w, n, second, first):
         return yb.at[pl.ds(w, n), h, second, first]
 
-    group = {0: 2, +1: 0, -1: 4}
-    s1 = {(h, dc, dp): net.slot() for h in (0, 1) for dc in (0, +1, -1) for dp in OFFSETS if (dc, dp) != (0, 0)}
-    order = ([(h, dc, 0) for h in (0, 1) for dc in (+1, -1)]
-             + [(h, dc, dp) for dp in (2, 1, 3) for h in (0, 1) for dc in (+1, -1, 0)])
-    for h, dc, dp in order:
-        net.copy(s1[h, dc, dp], mf_ref.at[:, 8 * h:8 * h + 8], at(h, group[dc], 2, mine[1 - h], mine[h]), dev(dc, h, dp))
+    def own(h):
+        return mf_ref.at[:, 8 * h:8 * h + 8]
+
+    w_mate, w_far = 4 * (1 - core), 4 * core
+    sl_own = {(h, dp): net.slot() for h in (0, 1) for dp in OFFSETS[1:]}
+    sl_mate = {(h, dp): net.slot() for h in (0, 1) for dp in OFFSETS}
+    sl_far = {(h, dp): net.slot() for h in (0, 1) for dp in OFFSETS}
+    hs = {(s, i): net.slot() for s in (+1, -1) for i in (0, 1)}
+
+    def far_copy(h, dp):
+        return pltpu.make_async_remote_copy(
+            src_ref=own(h), dst_ref=at(h, 4 * (1 - core), 2, mine[1 - h], mine[h]),
+            send_sem=net.send.at[sl_far[h, dp]], recv_sem=net.recv.at[sl_far[h, dp]],
+            device_id=dev(far, h, dp), device_id_type=MESH)
+
+    def blocks(s, i, k, a, e0, e1):
+        to = lax.rem(c + ncol + s, ncol)
+        return pltpu.make_async_remote_copy(
+            src_ref=hb_ref.at[k, e0:e1], dst_ref=hbuf.at[a, e0:e1], send_sem=net.send.at[hs[s, i]],
+            recv_sem=net.recv.at[hs[s, i]], device_id=(to, r), device_id_type=MESH)
+
+    def far_sends(on):
+        for dp in (2, 1, 3, 0):
+            for h in (0, 1):
+                far_copy(h, dp).start()
+        for gg in (0, 1):
+            @pl.when(gd == gg)
+            def _():
+                s = 2 * on - 1
+                for i, b in enumerate(BLOCKS[gg][s]):
+                    blocks(s, i, *b).start()
+
+    @pl.when(core == 1)
+    def _():
+        for d in cross(far):
+            greet(far_sem, d)
+        far_sends(1)
+    for dp in (2, 1, 3, 0):
+        for h in (0, 1):
+            net.copy(sl_mate[h, dp], own(h), at(h, 4 * core, 2, mine[1 - h], mine[h]), dev(mate, h, dp))
+            if dp:
+                net.copy(sl_own[h, dp], own(h), at(h, 2, 2, mine[1 - h], mine[h]), dev(c, h, dp))
     local = []
     for h in (0, 1):
-        l = pltpu.make_async_copy(mf_ref.at[:, 8 * h:8 * h + 8], at(h, 2, 2, mine[1 - h], mine[h]), loc.at[h])
+        l = pltpu.make_async_copy(own(h), at(h, 2, 2, mine[1 - h], mine[h]), loc.at[h])
         l.start()
         local.append(l)
-    hs = {(s, i): net.slot() for s in (+1, -1) for i in (0, 1)}
-
-    def blocks(s, i, k, a, e0, e1):
-        return pltpu.make_async_remote_copy(
-            src_ref=hb_ref.at[k, e0:e1], dst_ref=hbuf.at[a, e0:e1], send_sem=net.send.at[hs[s, i]],
-            recv_sem=net.recv.at[hs[s, i]], device_id=dev(s, 0, 0), device_id_type=MESH)
-
     for gg in (0, 1):
-        @pl.when(gd == gg)
-        def _():
-            for s in (+1, -1):
+        for on in (0, 1):
+            @pl.when((core == on) & (gd == gg))
+            def _():
+                s = 1 - 2 * on
                 for i, b in enumerate(BLOCKS[gg][s]):
                     blocks(s, i, *b).start()
 
@@ -120,35 +161,69 @@
             for i, (k, a, e0, e1) in enumerate(OWN[gg]):
                 pltpu.make_async_copy(hb_ref.at[k, e0:e1], hbuf.at[a, e0:e1], loc.at[2 + i]).start()
 
-    s2 = {(h, dp, s): net.slot() for h in (0, 1) for dp in OFFSETS for s in (+1, -1)}
-    s2r = {(h, dp, s): net.slot() for h in (0, 1) for dp in OFFSETS for s in (+1, -1)}
-    halves = {+1: (0, 3), -1: (3, 3)}
+    start = {0: 2 - 2 * core, 1: w_far}
+    half = {0: 2, 1: 1}
+    keys = [(u, h, s) for u in (0, 1) for h in (0, 1) for s in (+1, -1)]
+    s2 = {key + (p,): net.slot() for key in keys for p in (0, 1)}
+    s2r = {key: net.slot() for key in keys}
+    lead = {+1: 0, -1: 1}
 
     def place(h, dp):
-        return (mine[h] + 4 - dp) % SIDE
+        return lax.rem(mine[h] + 4 - dp, SIDE)
 
     def along(h, s):
-        return dev(0, 1 - h, s)
+        return dev(c, 1 - h, s)
 
     def second(h, s):
-        return (mine[1 - h] + 4 + s) % SIDE
-
-    for dp in OFFSETS:
-        for h in (0, 1):
-            if dp == 0:
-                local[h].wait()
-            for dc in (0, +1, -1):
-                if (dc, dp) != (0, 0):
-                    net.arrived(s1[h, dc, dp], at(h, group[dc], 2, mine[1 - h], place(h, dp)), dev(0, h, dp))
-            ref = at(h, 0, 6, mine[1 - h], place(h, dp))
+        return lax.rem(mine[1 - h] + 4 + s, SIDE)
+
+    def rows(u, h, p, q):
+        return yb.at[pl.ds(start[u] + p * half[u], half[u]), h, q]
+
+    def send2(u, h):
+        for first in (True, False):
             for s in (+1, -1):
-                net.copy(s2[h, dp, s], ref, ref, along(h, s))
-    for dp in OFFSETS:
-        for h in (0, 1):
-            for s in (+1, -1):
-                net.arrived(s2[h, dp, s], at(h, 0, 6, second(h, -s), place(h, dp)), along(h, -s))
-                ref = at(h, *halves[s], second(h, -s), place(h, dp))
-                net.copy(s2r[h, dp, s], ref, ref, along(h, s))
+                p = lead[s] if first else 1 - lead[s]
+                ref = rows(u, h, p, mine[1 - h])
+                net.copy(s2[u, h, s, p], ref, ref, along(h, s))
+
+    def relay2(u, h):
+        for s in (+1, -1):
+            ref = rows(u, h, lead[s], second(h, -s))
+            net.arrived(s2[u, h, s, lead[s]], ref, along(h, -s))
+            net.copy(s2r[u, h, s], ref, ref, along(h, s))
+
+    def last2(u, h):
+        for s in (+1, -1):
+            p = 1 - lead[s]
+            net.arrived(s2[u, h, s, p], rows(u, h, p, second(h, -s)), along(h, -s))
+            net.arrived(s2r[u, h, s], rows(u, h, lead[s], second(h, 2)), along(h, -s))
+
+    def answer(when):
+        @pl.when(when)
+        def _():
+            pl.semaphore_wait(far_sem, 7)
+            far_sends(0)
+
+    for h in (0, 1):
+        local[h].wait()
+        for dp in OFFSETS:
+            if dp:
+                net.arrived(sl_own[h, dp], at(h, 2, 2, mine[1 - h], place(h, dp)), along(h, 1))
+            net.arrived(sl_mate[h, dp], at(h, w_mate, 2, mine[1 - h], place(h, dp)), along(h, 1))
+        send2(0, h)
+    answer((core == 0) & (c > 0))
+    for h in (0, 1):
+        relay2(0, h)
+    for h in (0, 1):
+        for dp in OFFSETS:
+            net.arrived(sl_far[h, dp], at(h, w_far, 2, mine[1 - h], place(h, dp)), along(h, 1))
+        send2(1, h)
+    for h in (0, 1):
+        relay2(1, h)
+    for h in (0, 1):
+        last2(0, h)
+    answer(c == 0)
     for gg in (0, 1):
         @pl.when(g == gg)
         def _():
@@ -157,12 +232,14 @@
                     blocks(s, i, *b).wait_recv()
             for i, (k, a, e0, e1) in enumerate(OWN[gg]):
                 pltpu.make_async_copy(hb_ref.at[k, e0:e1], hbuf.at[a, e0:e1], loc.at[2 + i]).wait()
-    for dp in OFFSETS:
+    between()
+    for h in (0, 1):
+        last2(1, h)
+
+    def finish():
         for h in (0, 1):
-            for s in (+1, -1):
-                net.arrived(s2r[h, dp, s], at(h, *halves[s], second(h, 2), place(h, dp)), along(h, -s))
-
-    def finish():
+            for dp in OFFSETS:
+                far_copy(h, dp).wait_send()
         for gg in (0, 1):
             @pl.when(gd == gg)
             def _():
@@ -181,36 +258,40 @@
 
 
 def fused(ncol, mask_hbm, fermi_hbm, hb_ref, mf_ref, out_ref, yb, hbuf, h_ref, yt_ref, x_ref, eh_ref, el_ref,
-          stage, mask_ref, fermi_ref, send, recv, loc):
+          stage, mask_ref, fermi_ref, send, recv, loc, far_sem):
     c = lax.axis_index("cols")
     r = lax.axis_index("rep")
-    y, x = r // SIDE, r % SIDE
-    core = c % 2
-    g = (x * (1 - core) + y * core) % 2
-    gd = (x * core + y * (1 - core)) % 2
+    y, x = lax.div(r, SIDE), lax.rem(r, SIDE)
+    core = lax.rem(c, 2)
+    g = lax.rem(x * (1 - core) + y * core, 2)
+    gd = lax.rem(x * core + y * (1 - core), 2)
     other = r + (1 - 2 * g) * (1 + 3 * core)
     small = [pltpu.make_async_copy(mask_hbm, mask_ref, loc.at[4]), pltpu.make_async_copy(fermi_hbm, fermi_ref, loc.at[5])]
     for s in small:
         s.start()
     net = Net(send, recv)
-    finish = gather(ncol, c, r, g, gd, hb_ref, mf_ref, yb, hbuf, net, loc)
-    for s in small:
-        s.wait()
-    mask = [mask_ref[g, a].astype(F32) for a in range(NC)]
+    mask = []
+
+    def between():
+        for o in small:
+            o.wait()
+        mask.extend(mask_ref[g, a].astype(F32) for a in range(NC))
+        for a in range(NC):
+            for b in range(NC):
+                sl = (slice(a * B, (a + 1) * B), slice(b * B, (b + 1) * B))
+                if abs(a - b) <= 2:
+                    w = 0.5 * mask[a] * mask[b]
+                    h_ref[sl] = (hbuf[b, a - b + 2] + hbuf[a, b - a + 2].T) * w
+                else:
+                    h_ref[sl] = jnp.zeros((B, B), F32)
+
+    finish = gather(ncol, c, r, g, gd, hb_ref, mf_ref, yb, hbuf, net, loc, far_sem, between)
     mu = fermi_ref[0]
     ys = [yb[g + a].reshape(PS, B) * mask[a] for a in range(NC)]
     for a in range(NC):
         yt_ref[a * B:(a + 1) * B, :] = ys[a].T
     yt = split(yt_ref[...])
     yy = split(jnp.concatenate(ys, axis=1))
-    for a in range(NC):
-        for b in range(NC):
-            sl = (slice(a * B, (a + 1) * B), slice(b * B, (b + 1) * B))
-            if abs(a - b) <= 2:
-                w = 0.5 * mask[a] * mask[b]
-                h_ref[sl] = (hbuf[b, a - b + 2] + hbuf[a, b - a + 2].T) * w
-            else:
-                h_ref[sl] = jnp.zeros((B, B), F32)
     eye = lax.broadcasted_iota(jnp.int32, (PS, PS), 0) == lax.broadcasted_iota(jnp.int32, (PS, PS), 1)
     k = cdot(yy, yt)
     ks = split(k)
@@ -303,8 +384,9 @@
             pltpu.SemaphoreType.DMA((SLOTS,)),
             pltpu.SemaphoreType.DMA((SLOTS,)),
             pltpu.SemaphoreType.DMA((6,)),
+            pltpu.SemaphoreType.REGULAR,
         ],
-        compiler_params=pltpu.CompilerParams(collective_id=0, has_side_effects=True, vmem_limit_bytes=63 << 20),
+        compiler_params=pltpu.CompilerParams(collective_id=0, has_side_effects=True, vmem_limit_bytes=(107 << 19)),
     )(neighbour_mask, fermi_level, hamiltonian_band, margin_factors)
 
 

time: 42.8 us -> 40.6 us (0.949)
  Pallas kernels: 40.3 us -> 38.3 us
    pallas_call x1, Pallas kernels: 40.3 us -> 38.3 us  [on_device(): pl.pallas_call(functools.partial(fused, ncol), out_shape=jax.ShapeDtypeSt...]
    unnamed x1 -> x5, local copies, waits for them, and re-layouts: 1.62 us -> 1.41 us
where the time goes in v4:
time: 40.6 us; the launch traced here: 40.4 us
  Pallas kernels  38.3 us (94%)
  local copies, waits for them, and re-layouts  1.41 us (3%)
  between operations  0.68 us (2%)
    pallas_call x1, Pallas kernels, on_device(): pl.pallas_call(functools.partial(fused, ncol), out_shape=jax.ShapeDtypeSt...  38.3 us
    unnamed x5, local copies, waits for them, and re-layouts  1.41 us

profile of v4, /device:TPU:2, one launch (start us, length us, event | category | flops | bytes accessed | tf_op | source)
XLA Modules:
  0.0 40.4 jit_solution(16949113145409681981)
XLA Ops:
  0.0 0.0 copy-start.1
  0.7 0.0 copy-done.1
  0.7 0.0 copy-start
  0.7 0.7 %copy-done = f32[2,16,128]{2,1,0:T(8,128)S(1)} copy-done((f32[2,16,128]{2,1,0:T(8,128)S(1)}, f32[2,16,128]{2,1,0:T(8,128)}, u32[]{:S(2)}) %copy-start) | copy-done | bytes 16408
  1.4 38.3 %shard_map.46 = f32[2,40,640]{2,1,0:T(8,128)S(1)} custom-call(s32[2,5]{1,0:T(2,128)S(1)} %copy-done.1, f32[1]{0:T(128)S(6)} %copy.6.fermi_hbm, f32[2,5,128,128]{3,2,1,0:T(8,128)} %hb_ref.1, f32[2,16,128]{2,1,0:T(8,128)S(1)} %copy-done), custom_call_target="tpu_custom_call" | custom-call | tf_op jit(solution)/shard_map/pallas_call | solution.py:368
  39.7 0.7 %copy.7 = f32[2,40,640]{2,1,0:T(8,128)} copy(f32[2,40,640]{2,1,0:T(8,128)S(1)} %shard_map.46) | data formatting | bytes 409600
Async XLA Ops:
  0.0 0.7 %copy-start.1 = (s32[2,5]{1,0:T(2,128)S(1)}, s32[2,5]{1,0:T(2,128)}, u32[]{:S(2)}) copy-start(s32[2,5]{1,0:T(2,128)} %mask_hbm.1) | copy-start | bytes 124
  0.7 0.7 %copy-start = (f32[2,16,128]{2,1,0:T(8,128)S(1)}, f32[2,16,128]{2,1,0:T(8,128)}, u32[]{:S(2)}) copy-start(f32[2,16,128]{2,1,0:T(8,128)} %mf_ref.1) | copy-start | bytes 49156

commit v5 on v4

--- a/solution.py
+++ b/solution.py
@@ -61,14 +61,14 @@
 SLOTS = 64
 TILES = ((0, 256), (256, 512), (512, 640))
 BLOCKS = {
-    0: {+1: ((1, 1, 1, 5), (0, 0, 2, 5)), -1: ((0, 4, 0, 3),)},
+    0: {+1: ((1, 1, 1, 5), (0, 0, 2, 3), (0, 0, 3, 5)), -1: ((0, 4, 0, 3),)},
     1: {+1: ((1, 0, 2, 5),), -1: ((0, 3, 0, 4), (1, 4, 0, 3))},
 }
 OWN = {0: ((0, 2, 0, 5), (1, 3, 0, 4)), 1: ((1, 2, 0, 5), (0, 1, 1, 5))}
 OFFSETS = (0, 1, 3, 2)
 
 
-def gather(ncol, c, r, g, gd, hb_ref, mf_ref, yb, hbuf, net, loc, far_sem, between):
+def gather(ncol, c, r, g, gd, hb_ref, mf_ref, yb, hbuf, net, loc, near_sem, far_sem, yfar, between):
     y, x = lax.div(r, SIDE), lax.rem(r, SIDE)
     core = lax.rem(c, 2)
     mate = c + 1 - 2 * core
@@ -86,15 +86,20 @@
         pl.semaphore_signal(sem, inc=1, device_id=d, device_id_type=MESH)
 
     barrier = pltpu.get_barrier_semaphore()
-    near = cross(c)[1:] + cross(mate)
-    for d in near:
-        greet(barrier, d)
+    home = c - core
 
     @pl.when(core == 0)
     def _():
-        for d in cross(far):
+        for d in cross(c)[1:]:
             greet(barrier, d)
-    pl.semaphore_wait(barrier, len(near) + 7 * core)
+        for q in range(SIDE * SIDE):
+            greet(barrier, (far, q))
+
+    @pl.when(core == 1)
+    def _():
+        for d in cross(home):
+            greet(barrier, d)
+    pl.semaphore_wait(barrier, 13 + 3 * core)
 
     mine = {0: x, 1: y}
 
@@ -107,37 +112,52 @@
     w_mate, w_far = 4 * (1 - core), 4 * core
     sl_own = {(h, dp): net.slot() for h in (0, 1) for dp in OFFSETS[1:]}
     sl_mate = {(h, dp): net.slot() for h in (0, 1) for dp in OFFSETS}
-    sl_far = {(h, dp): net.slot() for h in (0, 1) for dp in OFFSETS}
-    hs = {(s, i): net.slot() for s in (+1, -1) for i in (0, 1)}
-
-    def far_copy(h, dp):
+    sl_far = [net.slot() for _ in range(SIDE * SIDE)]
+    got_far = sl_far[0]
+    hs = {(s, i): net.slot() for s in (+1, -1) for i in (0, 1, 2)}
+
+    def needed(to_core, gg):
+        return ((0, 2) if gg == 0 else (1, 2)) if to_core == 0 else ((0, 1) if gg == 0 else (0, 2))
+
+    def far_copy(on, q):
+        k0, k1 = needed(1 - on, q % 2 if on else q // SIDE % 2)
         return pltpu.make_async_remote_copy(
-            src_ref=own(h), dst_ref=at(h, 4 * (1 - core), 2, mine[1 - h], mine[h]),
-            send_sem=net.send.at[sl_far[h, dp]], recv_sem=net.recv.at[sl_far[h, dp]],
-            device_id=dev(far, h, dp), device_id_type=MESH)
-
-    def blocks(s, i, k, a, e0, e1):
+            src_ref=mf_ref.at[k0:k1], dst_ref=yfar.at[k0:k1, y, x],
+            send_sem=net.send.at[sl_far[q]], recv_sem=net.recv.at[got_far],
+            device_id=(far, q), device_id_type=MESH)
+
+    def blocks(s, i, k, a, e0, e1, shift=0):
         to = lax.rem(c + ncol + s, ncol)
         return pltpu.make_async_remote_copy(
             src_ref=hb_ref.at[k, e0:e1], dst_ref=hbuf.at[a, e0:e1], send_sem=net.send.at[hs[s, i]],
-            recv_sem=net.recv.at[hs[s, i]], device_id=(to, r), device_id_type=MESH)
-
-    def far_sends(on):
-        for dp in (2, 1, 3, 0):
-            for h in (0, 1):
-                far_copy(h, dp).start()
+            recv_sem=net.recv.at[hs[s, i]], device_id=(to, r - shift), device_id_type=MESH)
+
+    def far_blocks(on, op):
         for gg in (0, 1):
             @pl.when(gd == gg)
             def _():
                 s = 2 * on - 1
                 for i, b in enumerate(BLOCKS[gg][s]):
-                    blocks(s, i, *b).start()
+                    if (s, i) != (+1, 2):
+                        op(blocks(s, i, *b))
+                if (on, gg) == (1, 1):
+                    op(blocks(+1, 2, *BLOCKS[0][+1][2], shift=1))
+
+    def far_sends(on):
+        for q in range(SIDE * SIDE):
+            far_copy(on, q).start()
+        far_blocks(on, lambda d: d.start())
+
+    @pl.when(core == 0)
+    def _():
+        greet(near_sem, (mate, r))
 
     @pl.when(core == 1)
     def _():
-        for d in cross(far):
-            greet(far_sem, d)
+        for q in range(SIDE * SIDE):
+            greet(far_sem, (far, q))
         far_sends(1)
+        pl.semaphore_wait(near_sem, 1)
     for dp in (2, 1, 3, 0):
         for h in (0, 1):
             net.copy(sl_mate[h, dp], own(h), at(h, 4 * core, 2, mine[1 - h], mine[h]), dev(mate, h, dp))
@@ -163,7 +183,7 @@
 
     start = {0: 2 - 2 * core, 1: w_far}
     half = {0: 2, 1: 1}
-    keys = [(u, h, s) for u in (0, 1) for h in (0, 1) for s in (+1, -1)]
+    keys = [(u, h, s) for u in (0,) for h in (0, 1) for s in (+1, -1)]
     s2 = {key + (p,): net.slot() for key in keys for p in (0, 1)}
     s2r = {key: net.slot() for key in keys}
     lead = {+1: 0, -1: 1}
@@ -202,7 +222,7 @@
     def answer(when):
         @pl.when(when)
         def _():
-            pl.semaphore_wait(far_sem, 7)
+            pl.semaphore_wait(far_sem, SIDE * SIDE)
             far_sends(0)
 
     for h in (0, 1):
@@ -216,37 +236,47 @@
     for h in (0, 1):
         relay2(0, h)
     for h in (0, 1):
-        for dp in OFFSETS:
-            net.arrived(sl_far[h, dp], at(h, w_far, 2, mine[1 - h], place(h, dp)), along(h, 1))
-        send2(1, h)
-    for h in (0, 1):
-        relay2(1, h)
-    for h in (0, 1):
         last2(0, h)
     answer(c == 0)
-    for gg in (0, 1):
-        @pl.when(g == gg)
-        def _():
-            for s in (+1, -1):
-                for i, b in enumerate(BLOCKS[gg][s]):
-                    blocks(s, i, *b).wait_recv()
-            for i, (k, a, e0, e1) in enumerate(OWN[gg]):
-                pltpu.make_async_copy(hb_ref.at[k, e0:e1], hbuf.at[a, e0:e1], loc.at[2 + i]).wait()
-    between()
-    for h in (0, 1):
-        last2(1, h)
-
-    def finish():
-        for h in (0, 1):
-            for dp in OFFSETS:
-                far_copy(h, dp).wait_send()
+
+    def far_rows():
         for gg in (0, 1):
-            @pl.when(gd == gg)
+            for on in (0, 1):
+                @pl.when((core == on) & (g == gg))
+                def _():
+                    k0, k1 = needed(on, gg)
+                    net.arrived(got_far, yfar.at[k0:k1], (far, r))
+        for k in (0, 1):
+            yb[w_far + k, 0] = yfar[k, :, :, 0:8]
+            for p in range(SIDE):
+                for q in range(SIDE):
+                    yb[w_far + k, 1, p, q] = yfar[k, q, p, 8:16]
+
+    def far_band():
+        for gg in (0, 1):
+            @pl.when(g == gg)
             def _():
                 for s in (+1, -1):
                     for i, b in enumerate(BLOCKS[gg][s]):
-                        blocks(s, i, *b).wait_send()
-    return finish
+                        blocks(s, i, *b).wait_recv()
+                for i, (k, a, e0, e1) in enumerate(OWN[gg]):
+                    pltpu.make_async_copy(hb_ref.at[k, e0:e1], hbuf.at[a, e0:e1], loc.at[2 + i]).wait()
+        between()
+
+    def finish():
+        for on in (0, 1):
+            @pl.when(core == on)
+            def _():
+                for q in range(SIDE * SIDE):
+                    far_copy(on, q).wait_send()
+                far_blocks(on, lambda d: d.wait_send())
+                for gg in (0, 1):
+                    @pl.when(gd == gg)
+                    def _():
+                        s = 1 - 2 * on
+                        for i, b in enumerate(BLOCKS[gg][s]):
+                            blocks(s, i, *b).wait_send()
+    return far_rows, far_band, finish
 
 
 def cat3l(a, b):
@@ -258,7 +288,7 @@
 
 
 def fused(ncol, mask_hbm, fermi_hbm, hb_ref, mf_ref, out_ref, yb, hbuf, h_ref, yt_ref, x_ref, eh_ref, el_ref,
-          stage, mask_ref, fermi_ref, send, recv, loc, far_sem):
+          stage, yfar, mask_ref, fermi_ref, send, recv, loc, near_sem, far_sem):
     c = lax.axis_index("cols")
     r = lax.axis_index("rep")
     y, x = lax.div(r, SIDE), lax.rem(r, SIDE)
@@ -273,9 +303,6 @@
     mask = []
 
     def between():
-        for o in small:
-            o.wait()
-        mask.extend(mask_ref[g, a].astype(F32) for a in range(NC))
         for a in range(NC):
             for b in range(NC):
                 sl = (slice(a * B, (a + 1) * B), slice(b * B, (b + 1) * B))
@@ -285,7 +312,12 @@
                 else:
                     h_ref[sl] = jnp.zeros((B, B), F32)
 
-    finish = gather(ncol, c, r, g, gd, hb_ref, mf_ref, yb, hbuf, net, loc, far_sem, between)
+    far_rows, far_band, finish = gather(
+        ncol, c, r, g, gd, hb_ref, mf_ref, yb, hbuf, net, loc, near_sem, far_sem, yfar, between)
+    for o in small:
+        o.wait()
+    mask.extend(mask_ref[g, a].astype(F32) for a in range(NC))
+    far_rows()
     mu = fermi_ref[0]
     ys = [yb[g + a].reshape(PS, B) * mask[a] for a in range(NC)]
     for a in range(NC):
@@ -297,6 +329,7 @@
     ks = split(k)
     k2 = cdot(ks, ks)
     k3 = cdot(ks, split(k2))
+    far_band()
     pt = cdot(split(h_ref[...]), yt)
     n = cdot(yy, split(pt))
     one = jnp.ones((1, 1), F32)
@@ -379,12 +412,14 @@
             pltpu.VMEM((M, M), BF),
             pltpu.VMEM((M, M), BF),
             pltpu.VMEM((PIECE, M), F32),
+            pltpu.VMEM((2, SIDE, SIDE, 16, B), F32),
             pltpu.SMEM((2, NC), jnp.int32),
             pltpu.SMEM((1,), F32),
             pltpu.SemaphoreType.DMA((SLOTS,)),
             pltpu.SemaphoreType.DMA((SLOTS,)),
             pltpu.SemaphoreType.DMA((6,)),
             pltpu.SemaphoreType.REGULAR,
+            pltpu.SemaphoreType.REGULAR,
         ],
         compiler_params=pltpu.CompilerParams(collective_id=0, has_side_effects=True, vmem_limit_bytes=(107 << 19)),
     )(neighbour_mask, fermi_level, hamiltonian_band, margin_factors)

time: 40.6 us -> 37.8 us (0.931)
  the two profiles are of different devices: /device:TPU:2 before, /device:TPU:1 now
where the time goes in v5:
time: 37.8 us; the launch traced here: 37.6 us
  Pallas kernels  35.5 us (94%)
  local copies, waits for them, and re-layouts  1.41 us (4%)
  between operations  0.68 us (2%)
    pallas_call x1, Pallas kernels, on_device(): pl.pallas_call(functools.partial(fused, ncol), out_shape=jax.ShapeDtypeSt...  35.5 us
    unnamed x5, local copies, waits for them, and re-layouts  1.41 us

profile of v5, /device:TPU:1, one launch (start us, length us, event | category | flops | bytes accessed | tf_op | source)
XLA Modules:
  0.0 37.6 jit_solution(1149247628004483580)
XLA Ops:
  0.0 0.0 copy-start.1
  0.7 0.0 copy-done.1
  0.7 0.0 copy-start
  0.7 0.7 %copy-done = f32[2,16,128]{2,1,0:T(8,128)S(1)} copy-done((f32[2,16,128]{2,1,0:T(8,128)S(1)}, f32[2,16,128]{2,1,0:T(8,128)}, u32[]{:S(2)}) %copy-start) | copy-done | bytes 16408
  1.4 35.5 %shard_map.46 = f32[2,40,640]{2,1,0:T(8,128)S(1)} custom-call(s32[2,5]{1,0:T(2,128)S(1)} %copy-done.1, f32[1]{0:T(128)S(6)} %copy.6.fermi_hbm, f32[2,5,128,128]{3,2,1,0:T(8,128)} %hb_ref.1, f32[2,16,128]{2,1,0:T(8,128)S(1)} %copy-done), custom_call_target="tpu_custom_call" | custom-call | tf_op jit(solution)/shard_map/pallas_call | solution.py:401
  36.9 0.7 %copy.7 = f32[2,40,640]{2,1,0:T(8,128)} copy(f32[2,40,640]{2,1,0:T(8,128)S(1)} %shard_map.46) | data formatting | bytes 409600
Async XLA Ops:
  0.0 0.7 %copy-start.1 = (s32[2,5]{1,0:T(2,128)S(1)}, s32[2,5]{1,0:T(2,128)}, u32[]{:S(2)}) copy-start(s32[2,5]{1,0:T(2,128)} %mask_hbm.1) | copy-start | bytes 124
  0.7 0.7 %copy-start = (f32[2,16,128]{2,1,0:T(8,128)S(1)}, f32[2,16,128]{2,1,0:T(8,128)}, u32[]{:S(2)}) copy-start(f32[2,16,128]{2,1,0:T(8,128)} %mf_ref.1) | copy-start | bytes 49156

commit v6 on v5

--- a/solution.py
+++ b/solution.py
@@ -283,6 +283,10 @@
     return jnp.concatenate([a, b, a], axis=1)
 
 
+def vsum(e):
+    return jnp.sum(e.reshape(-1, 8, e.shape[1]), axis=0)
+
+
 def cdot(a, b):
     return dot(cat3l(*a), jnp.concatenate([b[0], b[0], b[1]], axis=0))
 
@@ -327,13 +331,13 @@
     eye = lax.broadcasted_iota(jnp.int32, (PS, PS), 0) == lax.broadcasted_iota(jnp.int32, (PS, PS), 1)
     k = cdot(yy, yt)
     ks = split(k)
-    k2 = cdot(ks, ks)
-    k3 = cdot(ks, split(k2))
     far_band()
     pt = cdot(split(h_ref[...]), yt)
+    k2 = cdot(ks, ks)
     n = cdot(yy, split(pt))
+    k3 = cdot(ks, split(k2))
     one = jnp.ones((1, 1), F32)
-    sumsq = M * one + 2.0 * jnp.sum(jnp.where(eye, k, 0.0), keepdims=True) + jnp.sum(k * k, keepdims=True)
+    sumsq = M * one + jnp.sum(vsum(jnp.where(eye, 2.0 * k, 0.0) + k * k), keepdims=True)
     cs = 2.0 * jnp.sqrt(sumsq / M)
     al = 1.0 / cs
     t = 0.5 * (3.0 - al)
@@ -348,22 +352,37 @@
     q3 = (0.25 * al * b2) * rs
     a0 = t * u * rs
     rm = q1 * k + q2 * k2 + q3 * k3 + jnp.where(eye, q0, 0.0)
-    vts = split(cdot(yt, split(rm)))
-    pts = split(a0 * pt + 0.5 * cdot(vts, split(n)))
+    rms = split(rm)
+    rn = split(0.5 * cdot(rms, split(n)))
+    both = cdot(yt, (jnp.concatenate([rms[0], rn[0]], axis=1), jnp.concatenate([rms[1], rn[1]], axis=1)))
+    vts = split(both[:, :PS])
+    pts = split(a0 * pt + both[:, PS:])
     a2 = a0 * a0
     lh, ll = (jnp.concatenate([pts[i], vts[i]], axis=1) for i in (0, 1))
     rh, rl = (jnp.concatenate([vts[i], pts[i]], axis=1) for i in (0, 1))
     lcat = cat3l(lh, ll)
     rcat = jnp.concatenate([rh, rh, rl], axis=1)
-    acc = jnp.zeros((1, 1), F32)
+
+    def put(e, p, q):
+        eh_ref[p:p + B, q:q + B], el_ref[p:p + B, q:q + B] = split(e)
+        x_ref[p:p + B, q:q + B] = e
+
+    total = jnp.zeros((8, B), F32)
+    eye = lax.broadcasted_iota(jnp.int32, (B, B), 0) == lax.broadcasted_iota(jnp.int32, (B, B), 1)
     for c0, c1 in TILES:
-        e = dot_nt(lcat, rcat[c0:c1]) + a2 * h_ref[:, c0:c1]
-        ii = lax.broadcasted_iota(jnp.int32, e.shape, 0)
-        jj = lax.broadcasted_iota(jnp.int32, e.shape, 1) + c0
-        e = e - jnp.where(ii == jj, mu, 0.0)
-        acc = acc + jnp.sum(e * e, keepdims=True)
-        eh_ref[:, c0:c1], el_ref[:, c0:c1] = split(e)
-        x_ref[:, c0:c1] = e
+        e = dot_nt(lcat[c0:], rcat[c0:c1]) + a2 * h_ref[c0:, c0:c1]
+        for p in range(c0, M, B):
+            for q in range(c0, c1, B):
+                block = e[p - c0:p - c0 + B, q - c0:q - c0 + B]
+                if p == q:
+                    block = block - jnp.where(eye, mu, 0.0)
+                if p >= c1:
+                    total = total + 2.0 * vsum(block * block)
+                    put(block.T, q, p)
+                else:
+                    total = total + vsum(block * block)
+                put(block, p, q)
+    acc = jnp.sum(total, keepdims=True)
     inv = 1.0 / (2.0 * jnp.sqrt(acc / M + 1e-5))
 
     def times(v, c0=0, c1=M):

time: 37.8 us -> 36.9 us (0.976)
  Pallas kernels: 35.5 us -> 34.6 us
    pallas_call x1, Pallas kernels: 35.5 us -> 34.6 us  [on_device(): pl.pallas_call(functools.partial(fused, ncol), out_shape=jax.ShapeDtypeSt...]
where the time goes in v6:
time: 36.9 us; the launch traced here: 36.7 us
  Pallas kernels  34.6 us (94%)
  local copies, waits for them, and re-layouts  1.41 us (4%)
  between operations  0.68 us (2%)
    pallas_call x1, Pallas kernels, on_device(): pl.pallas_call(functools.partial(fused, ncol), out_shape=jax.ShapeDtypeSt...  34.6 us
    unnamed x5, local copies, waits for them, and re-layouts  1.41 us

profile of v6, /device:TPU:1, one launch (start us, length us, event | category | flops | bytes accessed | tf_op | source)
XLA Modules:
  0.0 36.7 jit_solution(16619091607778320704)
XLA Ops:
  0.0 0.0 copy-start.1
  0.7 0.0 copy-done.1
  0.7 0.0 copy-start
  0.7 0.7 %copy-done = f32[2,16,128]{2,1,0:T(8,128)S(1)} copy-done((f32[2,16,128]{2,1,0:T(8,128)S(1)}, f32[2,16,128]{2,1,0:T(8,128)}, u32[]{:S(2)}) %copy-start) | copy-done | bytes 16408
  1.4 34.6 %shard_map.46 = f32[2,40,640]{2,1,0:T(8,128)S(1)} custom-call(s32[2,5]{1,0:T(2,128)S(1)} %copy-done.1, f32[1]{0:T(128)S(6)} %copy.6.fermi_hbm, f32[2,5,128,128]{3,2,1,0:T(8,128)} %hb_ref.1, f32[2,16,128]{2,1,0:T(8,128)S(1)} %copy-done), custom_call_target="tpu_custom_call" | custom-call | tf_op jit(solution)/shard_map/pallas_call | solution.py:420
  36.0 0.7 %copy.7 = f32[2,40,640]{2,1,0:T(8,128)} copy(f32[2,40,640]{2,1,0:T(8,128)S(1)} %shard_map.46) | data formatting | bytes 409600
Async XLA Ops:
  0.0 0.7 %copy-start.1 = (s32[2,5]{1,0:T(2,128)S(1)}, s32[2,5]{1,0:T(2,128)}, u32[]{:S(2)}) copy-start(s32[2,5]{1,0:T(2,128)} %mask_hbm.1) | copy-start | bytes 124
  0.7 0.7 %copy-start = (f32[2,16,128]{2,1,0:T(8,128)S(1)}, f32[2,16,128]{2,1,0:T(8,128)}, u32[]{:S(2)}) copy-start(f32[2,16,128]{2,1,0:T(8,128)} %mf_ref.1) | copy-start | bytes 49156

commit v7 on v6

--- a/solution.py
+++ b/solution.py
@@ -62,7 +62,7 @@
 TILES = ((0, 256), (256, 512), (512, 640))
 BLOCKS = {
     0: {+1: ((1, 1, 1, 5), (0, 0, 2, 3), (0, 0, 3, 5)), -1: ((0, 4, 0, 3),)},
-    1: {+1: ((1, 0, 2, 5),), -1: ((0, 3, 0, 4), (1, 4, 0, 3))},
+    1: {+1: ((1, 0, 2, 5),), -1: ((0, 3, 0, 4), (1, 4, 2, 3), (1, 4, 0, 2))},
 }
 OWN = {0: ((0, 2, 0, 5), (1, 3, 0, 4)), 1: ((1, 2, 0, 5), (0, 1, 1, 5))}
 OFFSETS = (0, 1, 3, 2)
@@ -99,7 +99,14 @@
     def _():
         for d in cross(home):
             greet(barrier, d)
-    pl.semaphore_wait(barrier, 13 + 3 * core)
+
+    inner = core * (1 - lax.div(c + 1, ncol))
+
+    @pl.when(inner == 1)
+    def _():
+        for q in range(1, SIDE * SIDE):
+            greet(barrier, (c, lax.rem(r + q, SIDE * SIDE)))
+    pl.semaphore_wait(barrier, 13 + 3 * core + 15 * inner)
 
     mine = {0: x, 1: y}
 
@@ -138,10 +145,12 @@
             def _():
                 s = 2 * on - 1
                 for i, b in enumerate(BLOCKS[gg][s]):
-                    if (s, i) != (+1, 2):
+                    if i < 2:
                         op(blocks(s, i, *b))
                 if (on, gg) == (1, 1):
                     op(blocks(+1, 2, *BLOCKS[0][+1][2], shift=1))
+                if (on, gg) == (0, 0):
+                    op(blocks(-1, 2, *BLOCKS[1][-1][2], shift=-SIDE))
 
     def far_sends(on):
         for q in range(SIDE * SIDE):
@@ -154,8 +163,12 @@
 
     @pl.when(core == 1)
     def _():
-        for q in range(SIDE * SIDE):
-            greet(far_sem, (far, q))
+        greet(far_sem, (far, r))
+
+        @pl.when(inner == 0)
+        def _():
+            for q in range(1, SIDE * SIDE):
+                greet(far_sem, (far, lax.rem(r + q, SIDE * SIDE)))
         far_sends(1)
         pl.semaphore_wait(near_sem, 1)
     for dp in (2, 1, 3, 0):
@@ -219,12 +232,13 @@
             net.arrived(s2[u, h, s, p], rows(u, h, p, second(h, -s)), along(h, -s))
             net.arrived(s2r[u, h, s], rows(u, h, lead[s], second(h, 2)), along(h, -s))
 
-    def answer(when):
+    def answer(when, answers):
         @pl.when(when)
         def _():
-            pl.semaphore_wait(far_sem, SIDE * SIDE)
+            pl.semaphore_wait(far_sem, answers)
             far_sends(0)
 
+    answer((core == 0) & (c > 0), 1)
     for h in (0, 1):
         local[h].wait()
         for dp in OFFSETS:
@@ -232,12 +246,11 @@
                 net.arrived(sl_own[h, dp], at(h, 2, 2, mine[1 - h], place(h, dp)), along(h, 1))
             net.arrived(sl_mate[h, dp], at(h, w_mate, 2, mine[1 - h], place(h, dp)), along(h, 1))
         send2(0, h)
-    answer((core == 0) & (c > 0))
     for h in (0, 1):
         relay2(0, h)
     for h in (0, 1):
         last2(0, h)
-    answer(c == 0)
+    answer(c == 0, SIDE * SIDE)
 
     def far_rows():
         for gg in (0, 1):

time: 36.9 us -> 35.5 us (0.962)
  the two profiles are of different devices: /device:TPU:1 before, /device:TPU:6 now
where the time goes in v7:
time: 35.5 us; the launch traced here: 35.3 us
  Pallas kernels  33.2 us (94%)
  local copies, waits for them, and re-layouts  1.41 us (4%)
  between operations  0.68 us (2%)
    pallas_call x1, Pallas kernels, on_device(): pl.pallas_call(functools.partial(fused, ncol), out_shape=jax.ShapeDtypeSt...  33.2 us
    unnamed x5, local copies, waits for them, and re-layouts  1.41 us

profile of v7, /device:TPU:6, one launch (start us, length us, event | category | flops | bytes accessed | tf_op | source)
XLA Modules:
  0.0 35.3 jit_solution(11750534404888240705)
XLA Ops:
  0.0 0.0 copy-start.1
  0.7 0.0 copy-done.1
  0.7 0.0 copy-start
  0.7 0.7 %copy-done = f32[2,16,128]{2,1,0:T(8,128)S(1)} copy-done((f32[2,16,128]{2,1,0:T(8,128)S(1)}, f32[2,16,128]{2,1,0:T(8,128)}, u32[]{:S(2)}) %copy-start) | copy-done | bytes 16408
  1.4 33.2 %shard_map.46 = f32[2,40,640]{2,1,0:T(8,128)S(1)} custom-call(s32[2,5]{1,0:T(2,128)S(1)} %copy-done.1, f32[1]{0:T(128)S(6)} %copy.6.fermi_hbm, f32[2,5,128,128]{3,2,1,0:T(8,128)} %hb_ref.1, f32[2,16,128]{2,1,0:T(8,128)S(1)} %copy-done), custom_call_target="tpu_custom_call" | custom-call | tf_op jit(solution)/shard_map/pallas_call | solution.py:433
  34.6 0.7 %copy.7 = f32[2,40,640]{2,1,0:T(8,128)} copy(f32[2,40,640]{2,1,0:T(8,128)S(1)} %shard_map.46) | data formatting | bytes 409600
Async XLA Ops:
  0.0 0.7 %copy-start.1 = (s32[2,5]{1,0:T(2,128)S(1)}, s32[2,5]{1,0:T(2,128)}, u32[]{:S(2)}) copy-start(s32[2,5]{1,0:T(2,128)} %mask_hbm.1) | copy-start | bytes 124
  0.7 0.7 %copy-start = (f32[2,16,128]{2,1,0:T(8,128)S(1)}, f32[2,16,128]{2,1,0:T(8,128)}, u32[]{:S(2)}) copy-start(f32[2,16,128]{2,1,0:T(8,128)} %mf_ref.1) | copy-start | bytes 49156

commit v8 on v7

--- a/solution.py
+++ b/solution.py
@@ -127,7 +127,7 @@
         return ((0, 2) if gg == 0 else (1, 2)) if to_core == 0 else ((0, 1) if gg == 0 else (0, 2))
 
     def far_copy(on, q):
-        k0, k1 = needed(1 - on, q % 2 if on else q // SIDE % 2)
+        k0, k1 = needed(1 - on, q // SIDE % 2 if on else q % 2)
         return pltpu.make_async_remote_copy(
             src_ref=mf_ref.at[k0:k1], dst_ref=yfar.at[k0:k1, y, x],
             send_sem=net.send.at[sl_far[q]], recv_sem=net.recv.at[got_far],
@@ -148,9 +148,9 @@
                     if i < 2:
                         op(blocks(s, i, *b))
                 if (on, gg) == (1, 1):
-                    op(blocks(+1, 2, *BLOCKS[0][+1][2], shift=1))
+                    op(blocks(+1, 2, *BLOCKS[0][+1][2], shift=SIDE))
                 if (on, gg) == (0, 0):
-                    op(blocks(-1, 2, *BLOCKS[1][-1][2], shift=-SIDE))
+                    op(blocks(-1, 2, *BLOCKS[1][-1][2], shift=-1))
 
     def far_sends(on):
         for q in range(SIDE * SIDE):
@@ -310,9 +310,9 @@
     r = lax.axis_index("rep")
     y, x = lax.div(r, SIDE), lax.rem(r, SIDE)
     core = lax.rem(c, 2)
-    g = lax.rem(x * (1 - core) + y * core, 2)
-    gd = lax.rem(x * core + y * (1 - core), 2)
-    other = r + (1 - 2 * g) * (1 + 3 * core)
+    g = lax.rem(y * (1 - core) + x * core, 2)
+    gd = lax.rem(y * core + x * (1 - core), 2)
+    other = r + (1 - 2 * g) * (4 - 3 * core)
     small = [pltpu.make_async_copy(mask_hbm, mask_ref, loc.at[4]), pltpu.make_async_copy(fermi_hbm, fermi_ref, loc.at[5])]
     for s in small:
         s.start()

time: 35.5 us -> 35.2 us (level)
  the two profiles are of different devices: /device:TPU:6 before, /device:TPU:1 now
where the time goes in v8:
time: 35.2 us; the launch traced here: 34.5 us
  Pallas kernels  32.4 us (92%)
  local copies, waits for them, and re-layouts  1.41 us (4%)
  between operations  0.68 us (2%)
    pallas_call x1, Pallas kernels, on_device(): pl.pallas_call(functools.partial(fused, ncol), out_shape=jax.ShapeDtypeSt...  32.4 us
    unnamed x5, local copies, waits for them, and re-layouts  1.41 us

profile of v8, /device:TPU:1, one launch (start us, length us, event | category | flops | bytes accessed | tf_op | source)
XLA Modules:
  0.0 34.5 jit_solution(2516629909316720350)
XLA Ops:
  0.0 0.0 copy-start.1
  0.7 0.0 copy-done.1
  0.7 0.0 copy-start
  0.7 0.7 %copy-done = f32[2,16,128]{2,1,0:T(8,128)S(1)} copy-done((f32[2,16,128]{2,1,0:T(8,128)S(1)}, f32[2,16,128]{2,1,0:T(8,128)}, u32[]{:S(2)}) %copy-start) | copy-done | bytes 16408
  1.4 32.4 %shard_map.46 = f32[2,40,640]{2,1,0:T(8,128)S(1)} custom-call(s32[2,5]{1,0:T(2,128)S(1)} %copy-done.1, f32[1]{0:T(128)S(6)} %copy.6.fermi_hbm, f32[2,5,128,128]{3,2,1,0:T(8,128)} %hb_ref.1, f32[2,16,128]{2,1,0:T(8,128)S(1)} %copy-done), custom_call_target="tpu_custom_call" | custom-call | tf_op jit(solution)/shard_map/pallas_call | solution.py:433
  33.8 0.7 %copy.7 = f32[2,40,640]{2,1,0:T(8,128)} copy(f32[2,40,640]{2,1,0:T(8,128)S(1)} %shard_map.46) | data formatting | bytes 409600
Async XLA Ops:
  0.0 0.7 %copy-start.1 = (s32[2,5]{1,0:T(2,128)S(1)}, s32[2,5]{1,0:T(2,128)}, u32[]{:S(2)}) copy-start(s32[2,5]{1,0:T(2,128)} %mask_hbm.1) | copy-start | bytes 124
  0.7 0.7 %copy-start = (f32[2,16,128]{2,1,0:T(8,128)S(1)}, f32[2,16,128]{2,1,0:T(8,128)}, u32[]{:S(2)}) copy-start(f32[2,16,128]{2,1,0:T(8,128)} %mf_ref.1) | copy-start | bytes 49156

commit v9 on v8

--- a/solution.py
+++ b/solution.py
@@ -238,7 +238,6 @@
             pl.semaphore_wait(far_sem, answers)
             far_sends(0)
 
-    answer((core == 0) & (c > 0), 1)
     for h in (0, 1):
         local[h].wait()
         for dp in OFFSETS:
@@ -246,6 +245,8 @@
                 net.arrived(sl_own[h, dp], at(h, 2, 2, mine[1 - h], place(h, dp)), along(h, 1))
             net.arrived(sl_mate[h, dp], at(h, w_mate, 2, mine[1 - h], place(h, dp)), along(h, 1))
         send2(0, h)
+        if h == 0:
+            answer((core == 0) & (c > 0), 1)
     for h in (0, 1):
         relay2(0, h)
     for h in (0, 1):

time: 35.2 us -> 35.7 us (1.014)
  the two profiles are of different devices: /device:TPU:1 before, /device:TPU:232 now
where the time goes in v9:
time: 35.7 us; the launch traced here: 35.5 us
  Pallas kernels  33.5 us (94%)
  local copies, waits for them, and re-layouts  1.41 us (4%)
  between operations  0.68 us (2%)
    pallas_call x1, Pallas kernels, on_device(): pl.pallas_call(functools.partial(fused, ncol), out_shape=jax.ShapeDtypeSt...  33.5 us
    unnamed x5, local copies, waits for them, and re-layouts  1.41 us

profile of v9, /device:TPU:232, one launch (start us, length us, event | category | flops | bytes accessed | tf_op | source)
XLA Modules:
  0.0 35.5 jit_solution(15176753158055754773)
XLA Ops:
  0.0 0.0 copy-start.1
  0.7 0.0 copy-done.1
  0.7 0.0 copy-start
  0.7 0.7 %copy-done = f32[2,16,128]{2,1,0:T(8,128)S(1)} copy-done((f32[2,16,128]{2,1,0:T(8,128)S(1)}, f32[2,16,128]{2,1,0:T(8,128)}, u32[]{:S(2)}) %copy-start) | copy-done | bytes 16408
  1.4 33.5 %shard_map.46 = f32[2,40,640]{2,1,0:T(8,128)S(1)} custom-call(s32[2,5]{1,0:T(2,128)S(1)} %copy-done.1, f32[1]{0:T(128)S(6)} %copy.6.fermi_hbm, f32[2,5,128,128]{3,2,1,0:T(8,128)} %hb_ref.1, f32[2,16,128]{2,1,0:T(8,128)S(1)} %copy-done), custom_call_target="tpu_custom_call" | custom-call | tf_op jit(solution)/shard_map/pallas_call | solution.py:434
  34.9 0.7 %copy.7 = f32[2,40,640]{2,1,0:T(8,128)} copy(f32[2,40,640]{2,1,0:T(8,128)S(1)} %shard_map.46) | data formatting | bytes 409600
Async XLA Ops:
  0.0 0.7 %copy-start.1 = (s32[2,5]{1,0:T(2,128)S(1)}, s32[2,5]{1,0:T(2,128)}, u32[]{:S(2)}) copy-start(s32[2,5]{1,0:T(2,128)} %mask_hbm.1) | copy-start | bytes 124
  0.7 0.7 %copy-start = (f32[2,16,128]{2,1,0:T(8,128)S(1)}, f32[2,16,128]{2,1,0:T(8,128)}, u32[]{:S(2)}) copy-start(f32[2,16,128]{2,1,0:T(8,128)} %mf_ref.1) | copy-start | bytes 49156
